TPU v7x, 32 devices: a whole 2x2x4 slice. The times are simulated.
32 devices in a mesh: slab: 2 (over x), inline: 8 (over z, y), xline: 2 (over core).
Axes of the slice: x: 2, y: 2, z: 4, core: 2. Of those that a mesh axis runs over, the one named last changes fastest.
Arguments:
- traces: bfloat16 [256, 48, 128], P(('slab', 'inline'), 'xline'), parts along dimension 0, may hold values from -15 to 15
- directions: int32 [10], replicated, may hold values from 0 to 31
- init_means: float32 [32, 20], replicated, may hold values from 0.3 to 2.5
- init_variances: float32 [32, 20], replicated, may hold values from 0.01 to 0.2
- init_weights: float32 [32], replicated, may hold values from 0.01 to 1
Outputs:
- posterior: bfloat16 [256, 32, 48, 128], P(('slab', 'inline'), None, 'xline'), parts along dimension 0
- final_means: float32 [64, 20], P('slab'), parts along dimension 0
- final_variances: float32 [64, 20], P('slab'), parts along dimension 0
- final_weights: float32 [64], P('slab'), parts along dimension 0
There are 2 independent parts, one for each index of `slab`. A program takes and returns all parts, laid end to end along the dimension named above; an argument that names none is the same for every part. Nothing has to cross between parts.
All inputs are finite; a program needn't handle non-finite values.
Results may differ from a plain program's by a relative error of at most 0.001.
The roundings to bfloat16 on the way count: a program that leaves them out, or rounds other values in their place, can miss the bound.
Values may be sent and summed in bfloat16 or wider, within the bound.
A program may use at most 64 MiB of HBM per device.

v0:
```python
import math

import jax
import jax.numpy as jnp
import numpy as np
from jax import lax
from jax.sharding import PartitionSpec as P

TAPS = 31
HALF = 15
AZIMUTHS = 8
DIPS = 4
ITERS = 2


eps_mag = 0.01
wavenumber = math.pi / 4.0
highest = lax.Precision.HIGHEST
cross_real = np.array([[[1.0, 0.0], [1.0, 0.0]], [[0.0, 1.0], [0.0, -1.0]]], np.float32)
cross_imag = np.array([[[0.0, 1.0], [0.0, 1.0]], [[-1.0, 0.0], [1.0, 0.0]]], np.float32)
inner_real = np.array([[1.0, 0.0], [0.0, 1.0]], np.float32)
inner_imag = np.array([[0.0, 1.0], [-1.0, 0.0]], np.float32)


def with_halo(cells, sides, width):
    for axis, dim in sides:
        count = lax.axis_size(axis)
        ends = count - 1
        head = lax.slice_in_dim(cells, 0, width, axis=dim)
        tail = lax.slice_in_dim(cells, cells.shape[dim] - width, cells.shape[dim], axis=dim)
        cells = jnp.concatenate(
            [
                lax.ppermute(tail, axis, [(i, (i + 1) % count) for i in range(ends)]),
                cells,
                lax.ppermute(head, axis, [((i + 1) % count, i) for i in range(ends)]),
            ],
            axis=dim,
        )
    return cells


def tap_table(directions):
    azimuth = (directions % AZIMUTHS).astype(jnp.float32) * (math.pi / AZIMUTHS)
    dip_angle = (directions // AZIMUTHS + 1).astype(jnp.float32) * (math.pi / (2 * DIPS + 2))
    wave_vector = wavenumber * jnp.stack(
        [
            jnp.sin(dip_angle) * jnp.cos(azimuth),
            jnp.sin(dip_angle) * jnp.sin(azimuth),
            jnp.cos(dip_angle),
        ],
        axis=1,
    )
    offsets = jnp.arange(TAPS).astype(jnp.float32) - HALF
    width_scale = HALF / 3.0
    envelope = jnp.exp(-offsets * offsets / (2.0 * width_scale * width_scale))
    envelope = envelope / jnp.sqrt(jnp.sum(envelope * envelope))
    phases = wave_vector[:, :, None] * offsets[None, None, :]
    return jnp.stack([envelope * jnp.cos(phases), envelope * jnp.sin(phases)], axis=2).astype(
        jnp.bfloat16
    )


def band_onehot(rows_in, rows_out, offset_base):
    difference = jnp.arange(rows_in)[:, None] - jnp.arange(rows_out)[None, :] + offset_base
    return (difference[:, :, None] == jnp.arange(TAPS)[None, None, :]).astype(jnp.float32)


def log_scores(feature_rows, centers, spreads, log_weights):
    inverse = 1.0 / spreads
    offset_term = log_weights - 0.5 * jnp.sum(jnp.log(2.0 * math.pi * spreads), axis=1)
    distance = jnp.sum(
        (feature_rows[None, :, :] - centers[:, :, None]) ** 2 * inverse[:, :, None], axis=1
    )
    return offset_term[:, None] - 0.5 * distance


def posterior_weights(feature_rows, centers, spreads, log_weights):
    scores = log_scores(feature_rows, centers, spreads, log_weights)
    largest = jnp.max(scores, axis=0, keepdims=True)
    exponent = jnp.exp(scores - largest)
    return exponent / jnp.sum(exponent, axis=0, keepdims=True)


def moment_pass(feature_rows, centers, spreads, log_weights):
    posterior = posterior_weights(feature_rows, centers, spreads, log_weights)
    return (
        posterior.astype(jnp.bfloat16),
        jnp.sum(posterior, axis=1),
        jnp.einsum("km,fm->kf", posterior, feature_rows, precision=highest),
        jnp.einsum("km,fm->kf", posterior, feature_rows * feature_rows, precision=highest),
    )


def per_device(traces, directions, init_means, init_variances, init_weights):
    rows_in, cols_in, samples = traces.shape
    orients = directions.shape[0]
    padded_rows = rows_in + 2 * HALF
    padded_cols = cols_in + 2 * HALF
    tap_values = tap_table(directions)
    wide_taps = tap_values.astype(jnp.float32)
    time_mats = jnp.einsum(
        "stn,orn->sort", band_onehot(samples, samples, HALF), wide_taps[:, 2], precision=highest
    )
    time_mats = time_mats.astype(jnp.bfloat16).reshape(samples, orients * 2 * samples)
    xline_taps = jnp.einsum("pqr,on->opqrn", cross_real, wide_taps[:, 1, 0]) + jnp.einsum(
        "pqr,on->opqrn", cross_imag, wide_taps[:, 1, 1]
    )
    xline_mats = jnp.einsum(
        "xyn,opqrn->oxpqry", band_onehot(padded_cols, cols_in, 0), xline_taps, precision=highest
    ).astype(jnp.bfloat16)
    inline_taps = jnp.einsum("rs,on->orsn", inner_real, wide_taps[:, 0, 0]) + jnp.einsum(
        "rs,on->orsn", inner_imag, wide_taps[:, 0, 1]
    )
    inline_mats = jnp.einsum(
        "ijn,orsn->oirsj", band_onehot(padded_rows, rows_in, 0), inline_taps, precision=highest
    ).astype(jnp.bfloat16)
    local_bands = jnp.dot(
        traces.reshape(rows_in * cols_in, samples), time_mats, preferred_element_type=jnp.float32
    )
    local_bands = local_bands.astype(jnp.bfloat16).reshape(rows_in, cols_in, orients * 2 * samples)
    wide_bands = with_halo(local_bands, (("inline", 0), ("xline", 1)), HALF)

    def orient_band(orient):
        picked = lax.dynamic_slice_in_dim(wide_bands, orient * 2 * samples, 2 * samples, 2)
        return picked.reshape(padded_rows, padded_cols, 2, samples)

    def orient_features(orient, buffer):
        band = orient_band(orient)
        across = jnp.einsum(
            "ixpt,xpqry->iqryt", band, xline_mats[orient], preferred_element_type=jnp.float32
        ).astype(jnp.bfloat16)
        inline_sum = jnp.einsum(
            "iqryt,irsj->jqsyt", across, inline_mats[orient], preferred_element_type=jnp.float32
        )
        magnitude = jnp.sqrt(
            inline_sum[:, :, 0] * inline_sum[:, :, 0]
            + inline_sum[:, :, 1] * inline_sum[:, :, 1]
            + eps_mag
        )
        return lax.dynamic_update_slice(
            buffer, magnitude.reshape(rows_in, 2, cols_in * samples), (0, 2 * orient, 0)
        )

    features = lax.fori_loop(
        0,
        orients,
        orient_features,
        jnp.zeros((rows_in, 2 * orients, cols_in * samples), jnp.float32),
    )
    total_cells = lax.axis_size("inline") * rows_in * lax.axis_size("xline") * cols_in * samples
    components = init_weights.shape[0]
    centers = init_means
    spreads = init_variances
    weights = init_weights
    log_weights = jnp.log(init_weights)
    posterior = None
    for iteration in range(ITERS):
        posterior, masses, firsts, seconds = lax.map(
            lambda feature_rows: moment_pass(feature_rows, centers, spreads, log_weights), features
        )
        total_mass, total_first, total_second = lax.psum(
            (jnp.sum(masses, axis=0), jnp.sum(firsts, axis=0), jnp.sum(seconds, axis=0)),
            ("inline", "xline"),
        )
        new_centers = (total_first + centers) / (total_mass + 1.0)[:, None]
        centred_sum = (
            total_second
            - 2.0 * new_centers * total_first
            + new_centers * new_centers * total_mass[:, None]
        )
        new_spreads = (centred_sum + spreads) / (total_mass + 1.0)[:, None]
        weights = (total_mass + 1.0) / (total_cells + components)
        log_weights = jnp.log(weights)
        centers = new_centers
        spreads = new_spreads
    return (posterior.reshape(rows_in, components, cols_in, samples), centers, spreads, weights)


def solution(mesh):
    in_specs = (P(("slab", "inline"), "xline", None), P(), P(), P(), P())
    out_specs = (
        P(("slab", "inline"), None, "xline", None),
        P("slab", None),
        P("slab", None),
        P("slab"),
    )
    return jax.shard_map(
        per_device, mesh=mesh, in_specs=in_specs, out_specs=out_specs, check_vma=False
    )
```

profile of v0, /device:TPU:0, one launch (start us, length us, event | category | flops | bytes accessed | tf_op | source)
XLA Modules:
  0.0 525.4 jit_solution(14991298293549350796)
XLA Ops:
  5.9 5.0 collective-permute-start
  12.8 76.9 %collective-permute-done = bf16[15,24,2560]{2,1,0:T(8,128)(2,1)S(1)} collective-permute-done((bf16[15,24,2560]{2,1,0:T(8,128)(2,1)S(1)}, bf16[15,24,2560]{2,1,0:T(8,128)(2,1)S(1)}, u32[]{:S(2)}, u32[]{:S(2)}) %collective-permute-start) | collective-permute-done | bytes 1843232 | tf_op jit(solution)/shard_map/ppermute | solution.py:33
  91.0 1.9 pad_maximum_fusion.1
  93.0 3.9 fusion.87
  96.9 3.1 collective-permute-start.2
  104.6 4.1 collective-permute-done.3
  108.7 8.8 %pad_maximum_fusion = bf16[46,54,2560]{2,0,1:T(8,128)(2,1)S(1)} fusion(bf16[46,15,2560]{2,0,1:T(8,128)(2,1)} %collective-permute-done.3, bf16[15,24,2560]{2,0,1:T(8,128)(2,1)} %copy-done.3, bf16[16,24,2560]{2,0,1:T(8,128)(2,1)S(1)} %copy.81, bf16[15,24,2560]{2,0,1:T(8,128)(2,1)} %copy-done.2, bf16[46,15,2560]{2,0,1:T(8,128)(2,1)} %collective-permute-done.2), kind=kLoop, calls=%fused_computation.56 | loop fusion | flops 63590400 | bytes 25436160 | tf_op jit(solution)/shard_map/concatenate | solution.py:31
  117.5 9.4 %copy.85 = bf16[46,54,2560]{2,1,0:T(8,128)(2,1)} copy(bf16[46,54,2560]{2,0,1:T(8,128)(2,1)S(1)} %pad_maximum_fusion) | data formatting | bytes 25436160 | tf_op jit(solution)/shard_map/while | solution.py:144
  126.9 2.7 broadcast_in_dim.24.clone
  129.6 53.1 %while.45 = (s32[]{:T(128)}, f32[16,20,3072]{2,1,0:T(8,128)}, bf16[10,46,2,2,16]{1,4,2,3,0:T(8,128)(2,1)S(1)}, bf16[10,54,2,2,2,24]{1,5,2,4,3,0:T(8,128)(2,1)S(1...) while((s32[]{:T(128)}, f32[16,20,3072]{2,1,0:T(8,128)}, ...), condition=%wide.region_2.3_spmd, body=%wide.region_1.2_spmd.sunk | while | flops 159227904 | bytes 13011161 | solution.py:144
  183.4 106.9 %while.46 = (s32[]{:T(128)}, f32[16,32]{1,0:T(8,128)S(1)}, f32[16,32,20]{1,2,0:T(8,128)S(1)}, f32[16,32,20]{1,2,0:T(8,128)}, f32[32,20]{0,1:T(8,128)S(1)}, /*ind...) while((s32[]{:T(128)}, f32[16,32]{1,0:T(8,128)S(1)}, ...), condition=%wide.region_9.10_spmd, body=%wide.region_3.9_spmd.sunk | while | flops 56975232 | bytes 3835885 | solution.py:158
  186.3 2.1 fusion.126
  192.9 2.1 fusion.126
  199.6 2.2 fusion.126
  206.3 2.2 fusion.126
  212.9 2.2 fusion.126
  219.6 2.2 fusion.126
  226.3 2.1 fusion.126
  232.9 2.2 fusion.126
  235.1 1.5 fusion.125
  239.6 2.2 fusion.126
  246.3 2.2 fusion.126
  253.0 2.2 fusion.126
  259.7 2.1 fusion.126
  266.3 2.1 fusion.126
  273.0 2.2 fusion.126
  279.7 2.1 fusion.126
  286.3 2.2 fusion.126
  291.4 61.6 %all-reduce.1 = (f32[32,20]{0,1:T(8,128)S(1)}, f32[32]{0:T(128)S(1)}, f32[32,20]{0,1:T(8,128)S(1)}) all-reduce(f32[32,20]{0,1:T(8,128)S(1)} %reduce_sum.137, f32[32]{0:T(128)S(1)} %reduce_sum.138, f32[32,20]{0,1:T(8,128)S(1)} %reduce_sum.136), channel_id=1, replica_groups=mesh['slab'=2,'inline'=8,'xline'=2] {'inline','xline'}, use_global_device_ids=true, to_apply=%region_13.14 | all-reduce | flops 1312 | bytes 10496 | tf_op jit(solution)/shard_map/psum | solution.py:161
  353.7 109.3 %while.47 = (s32[]{:T(128)}, bf16[16,32,3072]{2,1,0:T(8,128)(2,1)S(1)}, f32[16,32]{1,0:T(8,128)S(1)}, f32[16,32,20]{1,2,0:T(8,128)S(1)}, f32[16,32,20]{1,2,0:T(8...) while((s32[]{:T(128)}, ...), condition=%wide.region_22.23_spmd, body=%wide.region_16.22_spmd.sunk | while | flops 57466752 | bytes 4450809 | solution.py:158
  356.5 1.5 fusion.133
  358.0 2.2 fusion.134
  363.3 1.5 fusion.133
  364.9 2.2 fusion.134
  370.2 1.5 fusion.133
  371.7 2.2 fusion.134
  377.0 1.5 fusion.133
  378.5 2.2 fusion.134
  383.8 1.5 fusion.133
  385.4 2.2 fusion.134
  390.7 1.5 fusion.133
  392.2 2.2 fusion.134
  397.5 1.5 fusion.133
  399.0 2.2 fusion.134
  404.3 1.5 fusion.133
  405.9 2.2 fusion.134
  411.2 1.5 fusion.133
  412.7 2.2 fusion.134
  418.0 1.5 fusion.133
  419.5 2.2 fusion.134
  424.8 1.5 fusion.133
  426.4 2.2 fusion.134
  431.7 1.5 fusion.133
  433.2 2.2 fusion.134
  438.5 1.5 fusion.133
  440.1 2.2 fusion.134
  445.4 1.5 fusion.133
  446.9 2.2 fusion.134
  452.2 1.5 fusion.133
  453.7 2.2 fusion.134
  459.0 1.5 fusion.133
  460.6 2.2 fusion.134
  464.1 57.7 %all-reduce = (f32[32,20]{0,1:T(8,128)S(1)}, f32[32]{0:T(128)S(1)}, f32[32,20]{0,1:T(8,128)S(1)}) all-reduce(f32[32,20]{0,1:T(8,128)S(1)} %reduce_sum.139, f32[32]{0:T(128)S(1)} %reduce_sum.140, f32[32,20]{0,1:T(8,128)S(1)} %reduce_sum.141), channel_id=1, replica_groups=mesh['slab'=2,'inline'=8,'xline'=2] {'inline','xline'}, use_global_device_ids=true, to_apply=%region_24.25 | all-reduce | flops 1312 | bytes 10496 | tf_op jit(solution)/shard_map/psum | solution.py:161
  522.2 2.5 copy.111
  (436 shorter events, 189.1 us)
Async XLA Ops:
  0.6 4.3 copy-start
  5.9 83.8 %collective-permute-start = (bf16[15,24,2560]{2,1,0:T(8,128)(2,1)S(1)}, bf16[15,24,2560]{2,1,0:T(8,128)(2,1)S(1)}, u32[]{:S(2)}, u32[]{:S(2)}) collective-permute-start(bf16[15,24,2560]{2,1,0:T(8,128)(2,1)S(1)} %bitcast.205), channel_id=1, source_target_pairs={{0,2},{2,4},{4,6},{6,8},{8,10},{10,12},{12,14},{1,3},{3,5},{5,7},{... | collective-permute-start | bytes 5529608 | tf_op jit(solution)/shard_map/ppermute | solution.py:33
  10.9 79.4 %collective-permute-start.1 = (bf16[15,24,2560]{2,1,0:T(8,128)(2,1)S(1)}, bf16[15,24,2560]{2,1,0:T(8,128)(2,1)S(1)}, u32[]{:S(2)}, u32[]{:S(2)}) collective-permute-start(bf16[15,24,2560]{2,1,0:T(8,128)(2,1)S(1)} %bitcast.204), channel_id=1, source_target_pairs={{2,0},{4,2},{6,4},{8,6},{10,8},{12,10},{14,12},{3,1},{5,3},{7,5},{... | collective-permute-start | bytes 5529608 | tf_op jit(solution)/shard_map/ppermute | solution.py:35
  90.3 2.5 copy-start.2
  90.9 1.9 copy-start.3
  92.9 8.6 %copy-start.7 = (f32[2,2,2]{2,1,0:T(2,128)S(1)}, f32[2,2,2]{2,1,0:T(2,128)}, u32[]{:S(2)}) copy-start(f32[2,2,2]{2,1,0:T(2,128)} %constant.190.clone) | copy-start | bytes 100
  92.9 8.6 %copy-start.8 = (f32[2,2,2]{2,1,0:T(2,128)S(1)}, f32[2,2,2]{2,1,0:T(2,128)}, u32[]{:S(2)}) copy-start(f32[2,2,2]{2,1,0:T(2,128)} %constant.191.clone) | copy-start | bytes 100
  92.9 9.6 %copy-start.9 = (f32[2,2]{1,0:T(2,128)S(1)}, f32[2,2]{1,0:T(2,128)}, u32[]{:S(2)}) copy-start(f32[2,2]{1,0:T(2,128)} %constant.192.clone) | copy-start | bytes 52
  92.9 9.6 %copy-start.10 = (f32[2,2]{1,0:T(2,128)S(1)}, f32[2,2]{1,0:T(2,128)}, u32[]{:S(2)}) copy-start(f32[2,2]{1,0:T(2,128)} %constant.193.clone) | copy-start | bytes 52
  93.0 10.1 %copy-start.11 = (f32[32]{0:T(128)S(1)}, f32[32]{0:T(128)}, u32[]{:S(2)}) copy-start(f32[32]{0:T(128)} %param.19) | copy-start | bytes 388
  96.9 7.7 %collective-permute-start.2 = (bf16[46,15,2560]{2,0,1:T(8,128)(2,1)}, bf16[46,15,2560]{2,0,1:T(8,128)(2,1)}, u32[]{:S(2)}, u32[]{:S(2)}) collective-permute-start(bf16[46,15,2560]{2,0,1:T(8,128)(2,1)} %get-tuple-element.415), channel_id=1, source_target_pairs={{0,1},{2,3},{4,5},{6,7},{8,9},{10,11},{12,13},{14,15},{16,17},{18,... | collective-permute-start | bytes 10598408 | tf_op jit(solution)/shard_map/ppermute | solution.py:33
  100.0 8.7 %collective-permute-start.3 = (bf16[46,15,2560]{2,0,1:T(8,128)(2,1)}, bf16[46,15,2560]{2,0,1:T(8,128)(2,1)}, u32[]{:S(2)}, u32[]{:S(2)}) collective-permute-start(bf16[46,15,2560]{2,0,1:T(8,128)(2,1)} %get-tuple-element.416), channel_id=1, source_target_pairs={{1,0},{3,2},{5,4},{7,6},{9,8},{11,10},{13,12},{15,14},{17,16},{19,... | collective-permute-start | bytes 10598408 | tf_op jit(solution)/shard_map/ppermute | solution.py:35
  129.6 53.8 %copy-start.5 = (f32[32,20]{0,1:T(8,128)S(1)}, f32[32,20]{0,1:T(8,128)}, u32[]{:S(2)}) copy-start(f32[32,20]{0,1:T(8,128)} %param.18) | copy-start | bytes 7684
  129.6 53.8 %copy-start.6 = (f32[32,20]{0,1:T(8,128)S(1)}, f32[32,20]{0,1:T(8,128)}, u32[]{:S(2)}) copy-start(f32[32,20]{0,1:T(8,128)} %param.17) | copy-start | bytes 7684
  183.4 170.3 %copy-start.4 = (bf16[16,32,3072]{2,1,0:T(8,128)(2,1)S(1)}, bf16[16,32,3072]{2,1,0:T(8,128)(2,1)}, u32[]{:S(2)}) copy-start(bf16[16,32,3072]{2,1,0:T(8,128)(2,1)} %custom-call) | copy-start | bytes 9437188
  463.0 62.4 %copy-start.1 = (bf16[16,24,128]{2,1,0:T(8,128)(2,1)S(1)}, bf16[16,24,128]{2,1,0:T(8,128)(2,1)}, u32[]{:S(2)}) copy-start(bf16[16,24,128]{2,1,0:T(8,128)(2,1)} %param.15) | copy-start | bytes 294916
where the time goes:
time: 529 us; the launch traced here: 525 us
  matrix products  130 us (25%)
  blocking collectives  119 us (22%)
  local copies, waits for them, and re-layouts  97.6 us (18%)
  waiting for transfers between devices  82.5 us (16%)
  other arithmetic  81.9 us (15%)
  starting transfers between devices  10.9 us (2%)
    psum x2, blocking collectives, per_device(): lax.psum((jnp.sum(masses, axis=0), jnp.sum(firsts, axis=0), jnp.sum(secon...  119 us
    ppermute x2, waiting for transfers between devices, with_halo(): lax.ppermute(tail, axis, [(i, (i + 1) % count) for i in range(ends)])  78.4 us
    dot_general x32, matrix products, moment_pass(): jnp.einsum('km,fm->kf', posterior, feature_rows * feature_rows, precision...  69 us
    dot_general x32, matrix products, moment_pass(): jnp.einsum('km,fm->kf', posterior, feature_rows, precision=highest)  49 us
    reduce_sum x32, other arithmetic, log_scores(): jnp.sum((feature_rows[None, :, :] - centers[:, :, None]) ** 2 * inverse[:...  42.6 us
    sub x32, local copies, waits for them, and re-layouts, log_scores(): feature_rows[None, :, :] - centers[:, :, None]  31.7 us
    reshape x10, local copies, waits for them, and re-layouts, orient_band(): return picked.reshape(padded_rows, padded_cols, 2, samples)  15 us
    dynamic_slice x10, local copies, waits for them, and re-layouts, orient_band(): lax.dynamic_slice_in_dim(wide_bands, orient * 2 * samples, 2 * samples, 2)  14.1 us
  transfers between devices with their start and end apart: 4, of which 3 were waited for; matrix products, arithmetic and copies ran while one was open for 0% of the time, Pallas kernels for 0%

commit v1 on v0

v1 whole, which is shorter than its diff:
```python
import functools
import math

import jax
import jax.numpy as jnp
from jax import lax
from jax.experimental import pallas as pl
from jax.experimental.pallas import tpu as pltpu
from jax.sharding import PartitionSpec as P

TAPS = 31
HALF = 15
AZIMUTHS = 8
DIPS = 4
ITERS = 2
LANES = 128

eps_mag = 0.01
wavenumber = math.pi / 4.0
MESH = pl.DeviceIdType.MESH
f32 = jnp.float32
bf16 = jnp.bfloat16
VMEM = pltpu.MemorySpace.VMEM
SMEM = pltpu.MemorySpace.SMEM


def round_up(value, step):
    return -(-value // step) * step


def tap_table(directions):
    azimuth = (directions % AZIMUTHS).astype(f32) * (math.pi / AZIMUTHS)
    dip_angle = (directions // AZIMUTHS + 1).astype(f32) * (math.pi / (2 * DIPS + 2))
    wave_vector = wavenumber * jnp.stack(
        [
            jnp.sin(dip_angle) * jnp.cos(azimuth),
            jnp.sin(dip_angle) * jnp.sin(azimuth),
            jnp.cos(dip_angle),
        ],
        axis=1,
    )
    offsets = jnp.arange(TAPS).astype(f32) - HALF
    width_scale = HALF / 3.0
    envelope = jnp.exp(-offsets * offsets / (2.0 * width_scale * width_scale))
    envelope = envelope / jnp.sqrt(jnp.sum(envelope * envelope))
    phases = wave_vector[:, :, None] * offsets[None, None, :]
    return jnp.stack([envelope * jnp.cos(phases), envelope * jnp.sin(phases)], axis=2)


def halo_kernel(inlines, xlines, own_ref, out_ref, send_sem, recv_sem):
    row = lax.axis_index("inline")
    col = lax.axis_index("xline")
    steps = [
        (side, shift)
        for side in (-1, 0, 1)
        for shift in range(xlines)
        if not (side == 0 and shift == 0)
    ]

    def there(side):
        if side == 0:
            return row >= 0
        return row > 0 if side < 0 else row < inlines - 1

    def peer(side, shift):
        return {"inline": row + side, "xline": lax.rem(col + shift, xlines)}

    barrier = pltpu.get_barrier_semaphore()
    for side, shift in steps:
        @pl.when(there(side))
        def _(side=side, shift=shift):
            pl.semaphore_signal(barrier, inc=1, device_id=peer(side, shift), device_id_type=MESH)
    sides = 1 + (row > 0).astype(jnp.int32) + (row < inlines - 1).astype(jnp.int32)
    pl.semaphore_wait(barrier, sides * xlines - 1)

    def copy(side, shift):
        return pltpu.make_async_remote_copy(
            src_ref=own_ref,
            dst_ref=out_ref.at[1 - side, col],
            send_sem=send_sem.at[1 - side, shift],
            recv_sem=recv_sem.at[1 - side, shift],
            device_id=peer(side, shift),
            device_id_type=MESH,
        )

    for side, shift in steps:
        @pl.when(there(side))
        def _(side=side, shift=shift):
            copy(side, shift).start()
    out_ref[1, col] = own_ref[...]
    for side in (-1, 1):
        @pl.when(jnp.logical_not(there(side)))
        def _(side=side):
            out_ref[1 + side] = jnp.zeros(out_ref.shape[1:], out_ref.dtype)
    for side, shift in steps:
        @pl.when(there(side))
        def _(side=side, shift=shift):
            copy(side, shift).wait_send()
        @pl.when(there(-side))
        def _(side=side, shift=shift):
            copy(side, shift).wait_recv()


def gather_halo(traces):
    inlines, xlines = lax.axis_size("inline"), lax.axis_size("xline")
    return pl.pallas_call(
        functools.partial(halo_kernel, inlines, xlines),
        out_shape=jax.ShapeDtypeStruct((3, xlines) + traces.shape, traces.dtype),
        in_specs=[pl.BlockSpec(memory_space=VMEM)],
        out_specs=pl.BlockSpec(memory_space=VMEM),
        scratch_shapes=[
            pltpu.SemaphoreType.DMA((3, xlines)),
            pltpu.SemaphoreType.DMA((3, xlines)),
        ],
        compiler_params=pltpu.CompilerParams(collective_id=0, has_side_effects=True),
        name="halo",
    )(traces)


def filter_kernel(sizes, taps_ref, place_ref, halo_ref, out_ref, flat, cross):
    rows, cols, width, pad, orients = sizes
    deep = 3 * rows
    group = 4 if deep % 4 == 0 else 1
    orient = pl.program_id(0)

    @pl.when(orient == 0)
    def _():
        for block in range(3):
            for i in range(rows):
                for part in range(width // cols):
                    start = ((block * rows + i) * width) + part * cols
                    flat[start : start + cols, :] = halo_ref[block, part, i].astype(f32)
        for y in range(cols):
            for extra in range(pad - 2 * orients):
                out_ref[y, pl.ds(2 * orients + extra, rows, stride=pad), :] = jnp.full(
                    (rows, LANES), 1.0 if extra == 0 else 0.0, f32
                )

    def tap(axis, part, n):
        return taps_ref[((orient * 3 + axis) * 2 + part) * TAPS + n]

    def toeplitz(axis, difference):
        real = jnp.zeros(difference.shape, f32)
        imag = jnp.zeros(difference.shape, f32)
        for n in range(TAPS):
            hit = difference == n
            real = jnp.where(hit, tap(axis, 0, n), real)
            imag = jnp.where(hit, tap(axis, 1, n), imag)
        return real, imag

    def iotas(shape):
        return (
            lax.broadcasted_iota(jnp.int32, shape, 0),
            lax.broadcasted_iota(jnp.int32, shape, 1),
        )

    source, target = iotas((LANES, LANES))
    real, imag = toeplitz(2, source - target + HALF)
    time_mat = jnp.concatenate([real, imag], axis=1).astype(bf16)

    lanes = 2 * LANES
    y, x = iotas((cols, lanes))
    difference = jnp.where(x < width, x - y - place_ref[0] + HALF, -1)
    real, imag = toeplitz(1, difference)
    base = jnp.concatenate([real, imag], axis=0)
    x_mat = jnp.concatenate(
        [base if g == 0 else pltpu.roll(base, g * width, 1) for g in range(group)], axis=0
    ).astype(bf16)[:, : group * width]

    j, i = iotas((rows, lanes))
    real_first, imag_first = toeplitz(0, jnp.where(i < deep, i - j - rows + HALF, -1))
    real_next, imag_next = pltpu.roll(real_first, deep, 1), pltpu.roll(imag_first, deep, 1)
    base = jnp.concatenate([real_first - imag_next, imag_first + real_next], axis=0)
    i_mat = jnp.concatenate([base, pltpu.roll(base, 2 * deep, 1)], axis=0).astype(bf16)
    i_mat = i_mat[:, : 4 * deep]

    for step in range(deep // group):
        span = group * width
        band = jnp.dot(
            flat[step * span : (step + 1) * span, :].astype(bf16),
            time_mat,
            preferred_element_type=f32,
        ).astype(bf16)
        mixed = jnp.dot(x_mat, band, preferred_element_type=f32)
        for g in range(group):
            i_row = step * group + g
            first = g * 2 * cols
            with_cos = mixed[first : first + cols]
            with_sin = mixed[first + cols : first + 2 * cols]
            cu, cv = with_cos[:, :LANES], with_cos[:, LANES:]
            su, sv = with_sin[:, :LANES], with_sin[:, LANES:]
            for slot, value in enumerate((cu - sv, su + cv, cu + sv, su - cv)):
                cross[pl.ds(slot * cols * deep + i_row, cols, stride=deep), :] = value

    half = cols // 2
    for q in range(2):
        for y0 in range(0, half, 2):
            columns = []
            for dy in range(2):
                pieces = []
                for g in range(2):
                    for r in range(2):
                        start = ((q * 2 + r) * cols + y0 + dy + g * half) * deep
                        pieces.append(cross[start : start + deep, :])
                columns.append(jnp.concatenate(pieces, axis=0).astype(bf16))
            total = jnp.dot(i_mat, jnp.concatenate(columns, axis=1), preferred_element_type=f32)
            for g in range(2):
                re = total[g * 2 * rows : g * 2 * rows + rows]
                im = total[g * 2 * rows + rows : (g + 1) * 2 * rows]
                size = jnp.sqrt(re * re + im * im + eps_mag)
                for dy in range(2):
                    out_ref[
                        y0 + dy + g * half, pl.ds(2 * orient + q, rows, stride=pad), :
                    ] = size[:, dy * LANES : (dy + 1) * LANES]


def filter_features(halo, taps, place, pad):
    _, xlines, rows, cols, samples = halo.shape
    orients = taps.shape[0]
    width = xlines * cols
    sizes = (rows, cols, width, pad, orients)
    return pl.pallas_call(
        functools.partial(filter_kernel, sizes),
        out_shape=jax.ShapeDtypeStruct((cols, rows * pad, samples), f32),
        grid=(orients,),
        in_specs=[
            pl.BlockSpec(memory_space=SMEM),
            pl.BlockSpec(memory_space=SMEM),
            pl.BlockSpec(halo.shape, lambda o: (0,) * 5),
        ],
        out_specs=pl.BlockSpec((cols, rows * pad, samples), lambda o: (0, 0, 0)),
        scratch_shapes=[
            pltpu.VMEM((3 * rows * width, samples), f32),
            pltpu.VMEM((4 * cols * 3 * rows, samples), f32),
        ],
        compiler_params=pltpu.CompilerParams(vmem_limit_bytes=50 << 20),
        name="filters",
    )(taps.reshape(-1), place, halo)


def split3(value):
    high = value.astype(bf16)
    rest = value - high.astype(f32)
    mid = rest.astype(bf16)
    low = (rest - mid.astype(f32)).astype(bf16)
    return high, mid, low


def moment_kernel(sizes, with_posterior, feat_ref, shift_ref, mean_ref, var_ref, weight_ref, *rest):
    cols, pad, count, chunk = sizes
    if with_posterior:
        moment_ref, post_ref, table, total, wide = rest
    else:
        moment_ref, table, total = rest
    step = pl.program_id(0)
    comps = mean_ref.shape[0]

    @pl.when(step == 0)
    def _():
        lane = lax.broadcasted_iota(jnp.int32, (comps, 2 * LANES), 1)
        means = jnp.concatenate([mean_ref[...], jnp.zeros((comps, LANES), f32)], axis=1)
        spreads = jnp.concatenate([var_ref[...], jnp.ones((comps, LANES), f32)], axis=1)
        used = lane < count
        inverse = jnp.where(used, 1.0 / spreads, 0.0)
        scaled = means * inverse
        terms = jnp.where(used, jnp.log(2.0 * math.pi * spreads) + means * scaled, 0.0)
        constant = jnp.log(weight_ref[:, :1]) - 0.5 * jnp.sum(terms, axis=1, keepdims=True)
        row = jnp.where(used, scaled, 0.0) + jnp.where(lane == count, constant, 0.0)
        row = row + pltpu.roll(-0.5 * inverse, pad, 1)
        parts = split3(row)
        for index, part in enumerate(parts):
            part = part.astype(f32)
            tiled = part + pltpu.roll(part, 2 * pad, 1) + pltpu.roll(part, 4 * pad, 1)
            table[index * comps : (index + 1) * comps, :] = tiled.astype(bf16)
        total[...] = jnp.zeros_like(total)

    weights = table[:, : 6 * pad]
    for first in range(0, cols, chunk):
        values = jnp.concatenate(
            [feat_ref[first + y] - shift_ref[...] for y in range(chunk)], axis=1
        )
        both = jnp.concatenate([values, values * values], axis=0)
        operand = jnp.concatenate(split3(both), axis=0)
        wide_score = jnp.dot(weights, operand, preferred_element_type=f32)
        score = wide_score[:comps] + (
            wide_score[comps : 2 * comps] + wide_score[2 * comps : 3 * comps]
        )
        exponent = jnp.exp(score - jnp.max(score, axis=0, keepdims=True))
        share = exponent * (1.0 / jnp.sum(exponent, axis=0, keepdims=True))
        high = share.astype(bf16)
        low = (share - high.astype(f32)).astype(bf16)
        total[...] += lax.dot_general(
            jnp.concatenate([high, low], axis=0),
            operand,
            (((1,), (1,)), ((), ())),
            preferred_element_type=f32,
        )
        if with_posterior:
            for y in range(chunk):
                wide[pl.ds(first + y, comps, stride=cols), :] = share[
                    :, y * LANES : (y + 1) * LANES
                ]
    if with_posterior:
        for k in range(comps):
            post_ref[0, k] = wide[k * cols : (k + 1) * cols, :].astype(bf16)

    @pl.when(step == pl.num_programs(0) - 1)
    def _():
        both = total[:comps] + total[comps:]
        both = jnp.concatenate([both, jnp.zeros((comps, 2 * LANES - 6 * pad), f32)], axis=1)
        folded = (
            both
            + pltpu.roll(both, 2 * LANES - 2 * pad, 1)
            + pltpu.roll(both, 2 * LANES - 4 * pad, 1)
        )
        moment_ref[...] = folded[:, :LANES]


def moments(features, shift, params, count, rows, with_posterior):
    means, spreads, weights = params
    comps = means.shape[0]
    cols, flat, samples = features.shape
    pad = flat // rows
    chunk = 4 if cols % 4 == 0 else 1
    whole = lambda array: pl.BlockSpec(array.shape, lambda j: (0, 0))
    out_shape = [jax.ShapeDtypeStruct((comps, LANES), f32)]
    out_specs = [pl.BlockSpec((comps, LANES), lambda j: (0, 0))]
    scratch = [pltpu.VMEM((3 * comps, 2 * LANES), bf16), pltpu.VMEM((2 * comps, 6 * pad), f32)]
    if with_posterior:
        out_shape.append(jax.ShapeDtypeStruct((rows, comps, cols, samples), bf16))
        out_specs.append(pl.BlockSpec((1, comps, cols, samples), lambda j: (j, 0, 0, 0)))
        scratch.append(pltpu.VMEM((comps * cols, samples), f32))
    return pl.pallas_call(
        functools.partial(moment_kernel, (cols, pad, count, chunk), with_posterior),
        out_shape=out_shape,
        grid=(rows,),
        in_specs=[
            pl.BlockSpec((cols, pad, samples), lambda j: (0, j, 0)),
            whole(shift),
            whole(means),
            whole(spreads),
            whole(weights),
        ],
        out_specs=out_specs,
        scratch_shapes=scratch,
        compiler_params=pltpu.CompilerParams(vmem_limit_bytes=50 << 20),
        name="last_pass" if with_posterior else "first_pass",
    )(features, shift, means, spreads, weights)


def update_kernel(
    sizes, moment_ref, mean_ref, var_ref, mean_out, var_out, weight_out, slots, send_sem, recv_sem
):
    inlines, xlines, pad, count, cells = sizes
    members = inlines * xlines
    comps = mean_ref.shape[0]
    me = lax.axis_index("inline") * xlines + lax.axis_index("xline")

    def peer(shift):
        other = lax.rem(me + shift, members)
        return {"inline": other // xlines, "xline": lax.rem(other, xlines)}

    barrier = pltpu.get_barrier_semaphore()
    for shift in range(1, members):
        pl.semaphore_signal(barrier, inc=1, device_id=peer(shift), device_id_type=MESH)
    pl.semaphore_wait(barrier, members - 1)

    def copy(shift):
        return pltpu.make_async_remote_copy(
            src_ref=moment_ref,
            dst_ref=slots.at[me],
            send_sem=send_sem.at[shift],
            recv_sem=recv_sem.at[shift],
            device_id=peer(shift),
            device_id_type=MESH,
        )

    for shift in range(1, members):
        copy(shift).start()
    slots[me] = moment_ref[...]
    for shift in range(1, members):
        copy(shift).wait()
    total = slots[0]
    for member in range(1, members):
        total = total + slots[member]
    mass = total[:, count : count + 1]
    means, spreads = mean_ref[...], var_ref[...]
    used = lax.broadcasted_iota(jnp.int32, (comps, LANES), 1) < count
    first = jnp.where(used, total, 0.0)
    second = jnp.where(used, pltpu.roll(total, LANES - pad, 1), 0.0)
    below = mass + 1.0
    new_means = (first + means) / below
    centred = second - 2.0 * new_means * first + new_means * new_means * mass
    mean_out[...] = new_means
    var_out[...] = jnp.where(used, (centred + spreads) / below, 1.0)
    weight_out[...] = jnp.broadcast_to(below / (cells + comps), (comps, LANES))


def update(moment, params, pad, count, cells, collective_id):
    means, spreads, _ = params
    inlines, xlines = lax.axis_size("inline"), lax.axis_size("xline")
    members = inlines * xlines
    comps = means.shape[0]
    return pl.pallas_call(
        functools.partial(update_kernel, (inlines, xlines, pad, count, cells)),
        out_shape=[jax.ShapeDtypeStruct((comps, LANES), f32)] * 3,
        in_specs=[pl.BlockSpec(memory_space=VMEM)] * 3,
        out_specs=[pl.BlockSpec(memory_space=VMEM)] * 3,
        scratch_shapes=[
            pltpu.VMEM((members, comps, LANES), f32),
            pltpu.SemaphoreType.DMA((members,)),
            pltpu.SemaphoreType.DMA((members,)),
        ],
        compiler_params=pltpu.CompilerParams(
            collective_id=collective_id, has_side_effects=True
        ),
        name="update",
    )(moment, means, spreads)


def per_device(traces, directions, init_means, init_variances, init_weights):
    rows, cols, samples = traces.shape
    assert samples == LANES and rows >= HALF
    orients = directions.shape[0]
    count = 2 * orients
    pad = round_up(count + 1, 8)
    comps = init_weights.shape[0]
    cells = lax.axis_size("inline") * rows * lax.axis_size("xline") * cols * samples
    taps = tap_table(directions)
    place = (lax.axis_index("xline") * cols).astype(jnp.int32).reshape(1)
    shift_row = jnp.mean(init_means, axis=0)
    shift = jnp.broadcast_to(jnp.pad(shift_row, (0, pad - count))[:, None], (pad, LANES))
    halo = gather_halo(traces)
    features = filter_features(halo, taps, place, pad)
    means = jnp.pad(init_means - shift_row, ((0, 0), (0, LANES - count)))
    spreads = jnp.pad(init_variances, ((0, 0), (0, LANES - count)), constant_values=1.0)
    params = (means, spreads, jnp.broadcast_to(init_weights[:, None], (comps, LANES)))
    posterior = None
    for iteration in range(ITERS):
        last = iteration == ITERS - 1
        results = moments(features, shift, params, count, rows, last)
        if last:
            posterior = results[1]
        params = update(results[0], params, pad, count, cells, 1 + iteration)
    means, spreads, weights = params
    return posterior, means[:, :count] + shift_row, spreads[:, :count], weights[:, 0]


def solution(mesh):
    in_specs = (P(("slab", "inline"), "xline", None), P(), P(), P(), P())
    out_specs = (
        P(("slab", "inline"), None, "xline", None),
        P("slab", None),
        P("slab", None),
        P("slab"),
    )
    return jax.shard_map(
        per_device, mesh=mesh, in_specs=in_specs, out_specs=out_specs, check_vma=False
    )
```

time: 529 us -> 117 us (0.22)
  matrix products: 130 us -> 0 us
  blocking collectives: 119 us -> 0 us
  Pallas kernels: 0 us -> 99.7 us
  local copies, waits for them, and re-layouts: 97.6 us -> 10.4 us
  waiting for transfers between devices: 82.5 us -> 0 us
  other arithmetic: 81.9 us -> 4.21 us
  starting transfers between devices: 10.9 us -> 0 us
    dot_general x88 -> x0, matrix products: 130 us -> none  [the longest x32 69 us: moment_pass(): jnp.einsum('km,fm->kf', posterior, feature_rows * feature_rows, precision...]
    psum x2 -> x0, blocking collectives: 119 us -> none  [per_device(): lax.psum((jnp.sum(masses, axis=0), jnp.sum(firsts, axis=0), jnp.sum(secon...]
    pallas_call x0 -> x6, Pallas kernels: none -> 99.7 us  [the longest x2 34.9 us: moments(): pl.pallas_call(functools.partial(moment_kernel, (cols, pad, count, chunk)...]
    ppermute x4 -> x0, waiting for transfers between devices: 82.5 us -> none  [the longest x2 78.4 us: with_halo(): lax.ppermute(tail, axis, [(i, (i + 1) % count) for i in range(ends)])]
    reduce_sum x134 -> x1, other arithmetic: 59.6 us -> 0.82 us  [per_device(): shift_row = jnp.mean(init_means, axis=0)]
    sub x32 -> x0, local copies, waits for them, and re-layouts: 31.7 us -> none  [log_scores(): feature_rows[None, :, :] - centers[:, :, None]]
    reshape x11 -> x1, local copies, waits for them, and re-layouts: 15.6 us -> 0.13 us  [filter_features(): taps.reshape(-1)]
    dynamic_slice x10 -> x0, local copies, waits for them, and re-layouts: 14.1 us -> none  [orient_band(): lax.dynamic_slice_in_dim(wide_bands, orient * 2 * samples, 2 * samples, 2)]
  transfers between devices with their start and end apart: 4 -> 0, of which waited for: 3 -> 0; matrix products, arithmetic and copies ran while one was open for 0% -> 0% of each run, Pallas kernels for 0% -> 0%
where the time goes in v1:
time: 117 us; the launch traced here: 116 us
  Pallas kernels  99.7 us (85%)
  local copies, waits for them, and re-layouts  10.4 us (9%)
  other arithmetic  4.21 us (4%)
  between operations  1.46 us (1%)
    pallas_call x2, Pallas kernels, moments(): pl.pallas_call(functools.partial(moment_kernel, (cols, pad, count, chunk)...  34.9 us
    pallas_call x1, Pallas kernels, filter_features(): pl.pallas_call(functools.partial(filter_kernel, sizes), out_shape=jax.Sha...  27.7 us
    pallas_call x2, Pallas kernels, update(): pl.pallas_call(functools.partial(update_kernel, (inlines, xlines, pad, co...  23.3 us
    pallas_call x1, Pallas kernels, gather_halo(): pl.pallas_call(functools.partial(halo_kernel, inlines, xlines), out_shape...  13.8 us
    unnamed x20, local copies, waits for them, and re-layouts  8.05 us

profile of v1, /device:TPU:0, one launch (start us, length us, event | category | flops | bytes accessed | tf_op | source)
XLA Modules:
  0.0 115.8 jit_solution(16690355413675664268)
XLA Ops:
  0.6 0.6 multiply_reduce_fusion
  1.9 0.8 reduce_sum.19
  2.8 0.7 fusion.7
  3.5 0.7 multiply_bitcast_fusion.1
  4.2 0.1 cosine_bitcast_fusion
  4.3 0.1 copy.14
  4.4 0.1 broadcast_in_dim.4.shift_ref
  4.5 0.8 copy.16
  5.2 0.0 copy-start.1
  5.3 0.7 broadcast_in_dim.5.weight_ref
  6.0 0.8 copy.15
  6.8 0.0 copy-start.2
  6.8 0.5 fusion
  7.4 0.1 reshape.71.taps_ref
  7.5 13.8 %halo.1.halo_ref = bf16[3,2,16,24,128]{4,3,2,1,0:T(8,128)(2,1)} custom-call(bf16[16,24,128]{2,1,0:T(8,128)(2,1)} %own_ref.1), custom_call_target="tpu_custom_call" | custom-call | tf_op jit(solution)/shard_map/halo/pallas_call | solution.py:106
  21.3 0.0 copy-start
  21.3 1.1 copy-done
  22.3 27.7 %filters.1.feat_ref = f32[24,384,128]{2,1,0:T(8,128)} custom-call(f32[1860]{0:T(1024)S(1)} %reshape.71.taps_ref, s32[1]{0:T(128)} %bitcast.3.place_ref, bf16[3,2,16,24,128]{4,3,2,1,0:T(8,128)(2,1)S(1)} %copy-done), custom_call_target="tpu_custom_call" | custom-call | tf_op jit(solution)/shard_map/filters/pallas_call | solution.py:222
  50.1 16.7 %first_pass.1.moment_ref = f32[32,128]{1,0:T(8,128)S(1)} custom-call(f32[24,384,128]{2,1,0:T(8,128)} %filters.1.feat_ref, f32[24,128]{1,0:T(8,128)S(1)} %broadcast_in_dim.4.shift_ref, f32[32,128]{1,0:T(8,128)S(1)} %pad.13.mean_ref, f32[32,128]{1,0:T(8,128)S(1)} %pad.14.var_ref, f32[32,128]{1,0:T(8,128)S(1)} %broadcast_in_dim.5.weight_ref), custom_call_target="tpu_custom_call" | custom-call | tf_op jit(solution)/shard_map/first_pass/pallas_call | solution.py:333
  66.7 0.0 copy-done.1
  66.8 0.0 copy-done.2
  66.8 0.0 copy-start.5
  66.8 0.6 copy-done.5
  67.4 11.1 %update.2 = (f32[32,128]{1,0:T(8,128)}, f32[32,128]{1,0:T(8,128)}, f32[32,128]{1,0:T(8,128)}) custom-call(f32[32,128]{1,0:T(8,128)} %copy-done.5, f32[32,128]{1,0:T(8,128)} %copy-done.2, f32[32,128]{1,0:T(8,128)} %copy-done.1), custom_call_target="tpu_custom_call" | custom-call | tf_op jit(solution)/shard_map/update/pallas_call | solution.py:404
  78.4 0.0 copy-start.3
  78.5 0.7 copy-done.3
  79.2 0.0 copy-start.4
  79.2 0.7 copy-done.4
  79.9 0.0 copy-start.6
  79.9 0.7 copy-done.6
  80.6 18.2 %last_pass.1 = (f32[32,128]{1,0:T(8,128)S(1)}, bf16[16,32,24,128]{3,2,1,0:T(8,128)(2,1)}) custom-call(f32[24,384,128]{2,1,0:T(8,128)} %filters.1.feat_ref, f32[24,128]{1,0:T(8,128)S(1)} %broadcast_in_dim.4.shift_ref, f32[32,128]{1,0:T(8,128)S(1)} %copy-done.3, f32[32,128]{1,0:T(8,128)S(1)} %copy-done.4, f32[32,128]{1,0:T(8,128)S(1)} %copy-done.6), custom_call_target="tpu_custom_call" | custom-call | tf_op jit(solution)/shard_map/last_pass/pallas_call | solution.py:333
  98.8 0.0 copy-start.7
  98.8 0.6 copy-done.7
  99.4 12.3 %update.3 = (f32[32,128]{1,0:T(8,128)}, f32[32,128]{1,0:T(8,128)}, f32[32,128]{1,0:T(8,128)}) custom-call(f32[32,128]{1,0:T(8,128)} %copy-done.7, f32[32,128]{1,0:T(8,128)} %get-tuple-element.12.mean_ref, f32[32,128]{1,0:T(8,128)} %get-tuple-element.13.var_ref), custom_call_target="tpu_custom_call" | custom-call | tf_op jit(solution)/shard_map/update/pallas_call | solution.py:404
  111.7 0.7 slice_add_fusion
  112.4 0.7 copy.17
  113.1 1.4 %copy.18 = f32[32,20]{0,1:T(8,128)} copy(f32[32,20]{1,0:T(8,128)} %bitcast.8) | data formatting | bytes 5120
  114.5 1.3 %slice_reduce_fusion = f32[32]{0:T(128)} fusion(f32[32,128]{1,0:T(8,128)} %get-tuple-element.19), kind=kLoop, calls=%fused_computation.1 | loop fusion | bytes 256 | tf_op jit(solution)/shard_map/slice | solution.py:446
  (8 shorter events, 0.1 us)
Async XLA Ops:
  5.2 61.5 %copy-start.1 = (f32[32,128]{1,0:T(8,128)}, f32[32,128]{1,0:T(8,128)S(1)}, u32[]{:S(2)}) copy-start(f32[32,128]{1,0:T(8,128)S(1)} %pad.14.var_ref) | copy-start | bytes 49156
  6.8 60.0 %copy-start.2 = (f32[32,128]{1,0:T(8,128)}, f32[32,128]{1,0:T(8,128)S(1)}, u32[]{:S(2)}) copy-start(f32[32,128]{1,0:T(8,128)S(1)} %pad.13.mean_ref) | copy-start | bytes 49156
  21.3 1.1 copy-start
  66.8 0.6 copy-start.5
  78.4 0.7 copy-start.3
  79.2 0.7 copy-start.4
  79.9 0.7 copy-start.6
  98.8 0.6 copy-start.7

commit v2 on v1

--- a/solution.py
+++ b/solution.py
@@ -117,10 +117,10 @@
     )(traces)
 
 
-def filter_kernel(sizes, taps_ref, place_ref, halo_ref, out_ref, flat, cross):
+def filter_kernel(sizes, taps_ref, place_ref, halo_ref, out_ref, flat, x_mat, cross):
     rows, cols, width, pad, orients = sizes
     deep = 3 * rows
-    group = 4 if deep % 4 == 0 else 1
+    group = 8
     orient = pl.program_id(0)
 
     @pl.when(orient == 0)
@@ -129,7 +129,7 @@
             for i in range(rows):
                 for part in range(width // cols):
                     start = ((block * rows + i) * width) + part * cols
-                    flat[start : start + cols, :] = halo_ref[block, part, i].astype(f32)
+                    flat[start : start + cols, :] = halo_ref[block, part, i]
         for y in range(cols):
             for extra in range(pad - 2 * orients):
                 out_ref[y, pl.ds(2 * orients + extra, rows, stride=pad), :] = jnp.full(
@@ -154,21 +154,44 @@
             lax.broadcasted_iota(jnp.int32, shape, 1),
         )
 
-    source, target = iotas((LANES, LANES))
-    real, imag = toeplitz(2, source - target + HALF)
-    time_mat = jnp.concatenate([real, imag], axis=1).astype(bf16)
-
-    lanes = 2 * LANES
-    y, x = iotas((cols, lanes))
-    difference = jnp.where(x < width, x - y - place_ref[0] + HALF, -1)
-    real, imag = toeplitz(1, difference)
-    base = jnp.concatenate([real, imag], axis=0)
-    x_mat = jnp.concatenate(
-        [base if g == 0 else pltpu.roll(base, g * width, 1) for g in range(group)], axis=0
-    ).astype(bf16)[:, : group * width]
-
-    j, i = iotas((rows, lanes))
-    real_first, imag_first = toeplitz(0, jnp.where(i < deep, i - j - rows + HALF, -1))
+    def roll(value, amount):
+        return value if amount == 0 else pltpu.roll(value, amount, 1)
+
+    sub, lane = iotas((8, LANES))
+    bases = toeplitz(2, jnp.bitwise_and(sub - lane + HALF, LANES - 1))
+    pieces = []
+    for s in range(0, LANES, 8):
+        near = jnp.abs(sub + s - lane) <= HALF
+        pieces.append(
+            jnp.concatenate([jnp.where(near, roll(base, s), 0.0) for base in bases], axis=1)
+        )
+    time_mat = jnp.concatenate(pieces, axis=0).astype(bf16)
+
+    lanes = round_up(group * width + LANES, LANES)
+    sub, lane = iotas((group, lanes))
+    difference = lane - sub * width - place_ref[0] + HALF
+    bases = toeplitz(1, jnp.where(difference >= lanes - 64, difference - lanes, difference))
+    mine = jnp.logical_and(lane >= sub * width, lane < (sub + 1) * width)
+    for part in range(2):
+        for y in range(0, cols, 2):
+            pair = jnp.concatenate(
+                [jnp.where(mine, roll(bases[part], y + dy), 0.0) for dy in range(2)], axis=0
+            )
+            start = (part * cols + y) * group
+            x_mat[start : start + 2 * group, :] = pair[:, : group * width].astype(bf16)
+
+    sub, lane = iotas((8, LANES))
+    bases = toeplitz(0, jnp.bitwise_and(lane - sub - rows + HALF, LANES - 1))
+    real_first, imag_first = [
+        jnp.concatenate(
+            [jnp.where(lane < deep, roll(base, j), 0.0) for j in range(0, rows, 8)], axis=0
+        )
+        for base in bases
+    ]
+    blank = jnp.zeros((rows, LANES), f32)
+    real_first, imag_first = [
+        jnp.concatenate([part, blank], axis=1) for part in (real_first, imag_first)
+    ]
     real_next, imag_next = pltpu.roll(real_first, deep, 1), pltpu.roll(imag_first, deep, 1)
     base = jnp.concatenate([real_first - imag_next, imag_first + real_next], axis=0)
     i_mat = jnp.concatenate([base, pltpu.roll(base, 2 * deep, 1)], axis=0).astype(bf16)
@@ -177,20 +200,19 @@
     for step in range(deep // group):
         span = group * width
         band = jnp.dot(
-            flat[step * span : (step + 1) * span, :].astype(bf16),
+            flat[step * span : (step + 1) * span, :],
             time_mat,
             preferred_element_type=f32,
         ).astype(bf16)
-        mixed = jnp.dot(x_mat, band, preferred_element_type=f32)
-        for g in range(group):
-            i_row = step * group + g
-            first = g * 2 * cols
-            with_cos = mixed[first : first + cols]
-            with_sin = mixed[first + cols : first + 2 * cols]
+        mixed = jnp.dot(x_mat[...], band, preferred_element_type=f32)
+        for y in range(cols):
+            with_cos = mixed[y * group : (y + 1) * group]
+            with_sin = mixed[(cols + y) * group : (cols + y + 1) * group]
             cu, cv = with_cos[:, :LANES], with_cos[:, LANES:]
             su, sv = with_sin[:, :LANES], with_sin[:, LANES:]
             for slot, value in enumerate((cu - sv, su + cv, cu + sv, su - cv)):
-                cross[pl.ds(slot * cols * deep + i_row, cols, stride=deep), :] = value
+                start = (slot * cols + y) * deep + step * group
+                cross[start : start + group, :] = value
 
     half = cols // 2
     for q in range(2):
@@ -230,7 +252,8 @@
         ],
         out_specs=pl.BlockSpec((cols, rows * pad, samples), lambda o: (0, 0, 0)),
         scratch_shapes=[
-            pltpu.VMEM((3 * rows * width, samples), f32),
+            pltpu.VMEM((3 * rows * width, samples), bf16),
+            pltpu.VMEM((2 * cols * 8, 8 * width), bf16),
             pltpu.VMEM((4 * cols * 3 * rows, samples), f32),
         ],
         compiler_params=pltpu.CompilerParams(vmem_limit_bytes=50 << 20),
@@ -420,7 +443,7 @@
 
 def per_device(traces, directions, init_means, init_variances, init_weights):
     rows, cols, samples = traces.shape
-    assert samples == LANES and rows >= HALF
+    assert samples == LANES and rows >= HALF and rows % 8 == 0 and cols % 4 == 0
     orients = directions.shape[0]
     count = 2 * orients
     pad = round_up(count + 1, 8)

time: 117 us -> 112 us (0.957)
  Pallas kernels: 99.7 us -> 94.1 us
    pallas_call x1, Pallas kernels: 27.7 us -> 22.1 us  [filter_features(): pl.pallas_call(functools.partial(filter_kernel, sizes), out_shape=jax.Sha...]
where the time goes in v2:
time: 112 us; the launch traced here: 110 us
  Pallas kernels  94.1 us (84%)
  local copies, waits for them, and re-layouts  10.4 us (9%)
  other arithmetic  4.21 us (4%)
  between operations  1.46 us (1%)
    pallas_call x2, Pallas kernels, moments(): pl.pallas_call(functools.partial(moment_kernel, (cols, pad, count, chunk)...  34.9 us
    pallas_call x2, Pallas kernels, update(): pl.pallas_call(functools.partial(update_kernel, (inlines, xlines, pad, co...  23.3 us
    pallas_call x1, Pallas kernels, filter_features(): pl.pallas_call(functools.partial(filter_kernel, sizes), out_shape=jax.Sha...  22.1 us
    pallas_call x1, Pallas kernels, gather_halo(): pl.pallas_call(functools.partial(halo_kernel, inlines, xlines), out_shape...  13.8 us
    unnamed x20, local copies, waits for them, and re-layouts  8.05 us

profile of v2, /device:TPU:0, one launch (start us, length us, event | category | flops | bytes accessed | tf_op | source)
XLA Modules:
  0.0 110.2 jit_solution(716529256026036969)
XLA Ops:
  0.6 0.6 multiply_reduce_fusion
  1.9 0.8 reduce_sum.19
  2.8 0.7 fusion.7
  3.5 0.7 multiply_bitcast_fusion.1
  4.2 0.1 cosine_bitcast_fusion
  4.3 0.1 copy.14
  4.4 0.1 broadcast_in_dim.4.shift_ref
  4.5 0.8 copy.16
  5.2 0.0 copy-start.1
  5.3 0.7 broadcast_in_dim.5.weight_ref
  6.0 0.8 copy.15
  6.8 0.0 copy-start.2
  6.8 0.5 fusion
  7.4 0.1 reshape.71.taps_ref
  7.5 13.8 %halo.1.halo_ref = bf16[3,2,16,24,128]{4,3,2,1,0:T(8,128)(2,1)} custom-call(bf16[16,24,128]{2,1,0:T(8,128)(2,1)} %own_ref.1), custom_call_target="tpu_custom_call" | custom-call | tf_op jit(solution)/shard_map/halo/pallas_call | solution.py:106
  21.3 0.0 copy-start
  21.3 1.1 copy-done
  22.3 22.1 %filters.1.feat_ref = f32[24,384,128]{2,1,0:T(8,128)} custom-call(f32[1860]{0:T(1024)S(1)} %reshape.71.taps_ref, s32[1]{0:T(128)} %bitcast.3.place_ref, bf16[3,2,16,24,128]{4,3,2,1,0:T(8,128)(2,1)S(1)} %copy-done), custom_call_target="tpu_custom_call" | custom-call | tf_op jit(solution)/shard_map/filters/pallas_call | solution.py:244
  44.5 16.7 %first_pass.1.moment_ref = f32[32,128]{1,0:T(8,128)S(1)} custom-call(f32[24,384,128]{2,1,0:T(8,128)} %filters.1.feat_ref, f32[24,128]{1,0:T(8,128)S(1)} %broadcast_in_dim.4.shift_ref, f32[32,128]{1,0:T(8,128)S(1)} %pad.13.mean_ref, f32[32,128]{1,0:T(8,128)S(1)} %pad.14.var_ref, f32[32,128]{1,0:T(8,128)S(1)} %broadcast_in_dim.5.weight_ref), custom_call_target="tpu_custom_call" | custom-call | tf_op jit(solution)/shard_map/first_pass/pallas_call | solution.py:356
  61.1 0.0 copy-done.1
  61.2 0.0 copy-done.2
  61.2 0.0 copy-start.5
  61.2 0.6 copy-done.5
  61.8 11.1 %update.2 = (f32[32,128]{1,0:T(8,128)}, f32[32,128]{1,0:T(8,128)}, f32[32,128]{1,0:T(8,128)}) custom-call(f32[32,128]{1,0:T(8,128)} %copy-done.5, f32[32,128]{1,0:T(8,128)} %copy-done.2, f32[32,128]{1,0:T(8,128)} %copy-done.1), custom_call_target="tpu_custom_call" | custom-call | tf_op jit(solution)/shard_map/update/pallas_call | solution.py:427
  72.8 0.0 copy-start.3
  72.9 0.7 copy-done.3
  73.6 0.0 copy-start.4
  73.6 0.7 copy-done.4
  74.3 0.0 copy-start.6
  74.3 0.7 copy-done.6
  75.0 18.2 %last_pass.1 = (f32[32,128]{1,0:T(8,128)S(1)}, bf16[16,32,24,128]{3,2,1,0:T(8,128)(2,1)}) custom-call(f32[24,384,128]{2,1,0:T(8,128)} %filters.1.feat_ref, f32[24,128]{1,0:T(8,128)S(1)} %broadcast_in_dim.4.shift_ref, f32[32,128]{1,0:T(8,128)S(1)} %copy-done.3, f32[32,128]{1,0:T(8,128)S(1)} %copy-done.4, f32[32,128]{1,0:T(8,128)S(1)} %copy-done.6), custom_call_target="tpu_custom_call" | custom-call | tf_op jit(solution)/shard_map/last_pass/pallas_call | solution.py:356
  93.2 0.0 copy-start.7
  93.2 0.6 copy-done.7
  93.8 12.3 %update.3 = (f32[32,128]{1,0:T(8,128)}, f32[32,128]{1,0:T(8,128)}, f32[32,128]{1,0:T(8,128)}) custom-call(f32[32,128]{1,0:T(8,128)} %copy-done.7, f32[32,128]{1,0:T(8,128)} %get-tuple-element.12.mean_ref, f32[32,128]{1,0:T(8,128)} %get-tuple-element.13.var_ref), custom_call_target="tpu_custom_call" | custom-call | tf_op jit(solution)/shard_map/update/pallas_call | solution.py:427
  106.1 0.7 slice_add_fusion
  106.8 0.7 copy.17
  107.5 1.4 %copy.18 = f32[32,20]{0,1:T(8,128)} copy(f32[32,20]{1,0:T(8,128)} %bitcast.8) | data formatting | bytes 5120
  108.9 1.3 %slice_reduce_fusion = f32[32]{0:T(128)} fusion(f32[32,128]{1,0:T(8,128)} %get-tuple-element.19), kind=kLoop, calls=%fused_computation.1 | loop fusion | bytes 256 | tf_op jit(solution)/shard_map/slice | solution.py:469
  (8 shorter events, 0.1 us)
Async XLA Ops:
  5.2 55.9 %copy-start.1 = (f32[32,128]{1,0:T(8,128)}, f32[32,128]{1,0:T(8,128)S(1)}, u32[]{:S(2)}) copy-start(f32[32,128]{1,0:T(8,128)S(1)} %pad.14.var_ref) | copy-start | bytes 49156
  6.8 54.4 %copy-start.2 = (f32[32,128]{1,0:T(8,128)}, f32[32,128]{1,0:T(8,128)S(1)}, u32[]{:S(2)}) copy-start(f32[32,128]{1,0:T(8,128)S(1)} %pad.13.mean_ref) | copy-start | bytes 49156
  21.3 1.1 copy-start
  61.2 0.6 copy-start.5
  72.8 0.7 copy-start.3
  73.6 0.7 copy-start.4
  74.3 0.7 copy-start.6
  93.2 0.6 copy-start.7

commit v3 on v2

v3 whole, which is shorter than its diff:
```python
import functools
import math

import jax
import jax.numpy as jnp
from jax import lax
from jax.experimental import pallas as pl
from jax.experimental.pallas import tpu as pltpu
from jax.sharding import PartitionSpec as P

TAPS = 31
HALF = 15
AZIMUTHS = 8
DIPS = 4
LANES = 128

eps_mag = 0.01
wavenumber = math.pi / 4.0
width_scale = HALF / 3.0
norm = math.sqrt(
    sum(math.exp(-n * n / (width_scale * width_scale)) for n in range(-HALF, HALF + 1))
)
MESH = pl.DeviceIdType.MESH
f32 = jnp.float32
bf16 = jnp.bfloat16
VMEM = pltpu.MemorySpace.VMEM
SMEM = pltpu.MemorySpace.SMEM


def round_up(value, step):
    return -(-value // step) * step


def halo_kernel(inlines, xlines, own_ref, out_ref, send_sem, recv_sem):
    row = lax.axis_index("inline")
    col = lax.axis_index("xline")

    def there(side):
        return row > 0 if side < 0 else row < inlines - 1

    barrier = pltpu.get_barrier_semaphore()
    for side in (-1, 1):
        @pl.when(there(side))
        def _(side=side):
            pl.semaphore_signal(
                barrier, inc=1, device_id={"inline": row + side}, device_id_type=MESH
            )
    for shift in range(1, xlines):
        pl.semaphore_signal(
            barrier,
            inc=1,
            device_id={"xline": lax.rem(col + shift, xlines)},
            device_id_type=MESH,
        )
    sides = (row > 0).astype(jnp.int32) + (row < inlines - 1).astype(jnp.int32)
    pl.semaphore_wait(barrier, sides + xlines - 1)

    def along(side):
        return pltpu.make_async_remote_copy(
            src_ref=own_ref,
            dst_ref=out_ref.at[1 - side, col],
            send_sem=send_sem.at[1 - side, 0],
            recv_sem=recv_sem.at[1 - side, 0],
            device_id={"inline": row + side},
            device_id_type=MESH,
        )

    def across(block, shift):
        return pltpu.make_async_remote_copy(
            src_ref=own_ref if block == 1 else out_ref.at[block, col],
            dst_ref=out_ref.at[block, col],
            send_sem=send_sem.at[block, shift],
            recv_sem=recv_sem.at[block, shift],
            device_id={"xline": lax.rem(col + shift, xlines)},
            device_id_type=MESH,
        )

    for side in (-1, 1):
        @pl.when(there(side))
        def _(side=side):
            along(side).start()
    for shift in range(1, xlines):
        across(1, shift).start()
    out_ref[1, col] = own_ref[...]
    for side in (-1, 1):
        @pl.when(jnp.logical_not(there(side)))
        def _(side=side):
            out_ref[1 + side] = jnp.zeros(out_ref.shape[1:], out_ref.dtype)
    for side in (-1, 1):
        @pl.when(there(side))
        def _(side=side):
            along(-side).wait_recv()
            for shift in range(1, xlines):
                across(1 + side, shift).start()
    for shift in range(1, xlines):
        across(1, shift).wait()
    for side in (-1, 1):
        @pl.when(there(side))
        def _(side=side):
            along(side).wait_send()
            for shift in range(1, xlines):
                across(1 + side, shift).wait()


def gather_halo(traces):
    inlines, xlines = lax.axis_size("inline"), lax.axis_size("xline")
    return pl.pallas_call(
        functools.partial(halo_kernel, inlines, xlines),
        out_shape=jax.ShapeDtypeStruct((3, xlines) + traces.shape, traces.dtype),
        in_specs=[pl.BlockSpec(memory_space=VMEM)],
        out_specs=pl.BlockSpec(memory_space=VMEM),
        scratch_shapes=[
            pltpu.SemaphoreType.DMA((3, xlines)),
            pltpu.SemaphoreType.DMA((3, xlines)),
        ],
        compiler_params=pltpu.CompilerParams(collective_id=0, has_side_effects=True),
        name="halo",
    )(traces)


def filter_kernel(sizes, dir_ref, halo_ref, out_ref, flat, x_mat, cross):
    rows, cols, width, pad, orients = sizes
    deep = 3 * rows
    group = 8
    orient = pl.program_id(0)

    @pl.when(orient == 0)
    def _():
        for block in range(3):
            for i in range(rows):
                for part in range(width // cols):
                    start = ((block * rows + i) * width) + part * cols
                    flat[start : start + cols, :] = halo_ref[block, part, i]
        for y in range(cols):
            for extra in range(pad - 2 * orients):
                out_ref[y, pl.ds(2 * orients + extra, rows, stride=pad), :] = jnp.full(
                    (rows, LANES), 1.0 if extra == 0 else 0.0, f32
                )

    direction = dir_ref[orient]
    azimuth = jnp.full((8, LANES), (direction % AZIMUTHS).astype(f32)) * (math.pi / AZIMUTHS)
    dip_angle = jnp.full((8, LANES), (direction // AZIMUTHS + 1).astype(f32)) * (
        math.pi / (2 * DIPS + 2)
    )
    waves = [
        wavenumber * (jnp.sin(dip_angle) * jnp.cos(azimuth)),
        wavenumber * (jnp.sin(dip_angle) * jnp.sin(azimuth)),
        wavenumber * jnp.cos(dip_angle),
    ]

    def toeplitz(axis, difference):
        offset = (difference - HALF).astype(f32)
        copies = difference.shape[1] // LANES
        wave = waves[axis]
        phase = offset * (wave if copies == 1 else jnp.concatenate([wave] * copies, axis=1))
        envelope = jnp.exp(-offset * offset / (2.0 * width_scale * width_scale)) / norm
        hit = jnp.logical_and(difference >= 0, difference < TAPS)
        real = jnp.where(hit, envelope * jnp.cos(phase), 0.0)
        imag = jnp.where(hit, envelope * jnp.sin(phase), 0.0)
        return real, imag

    def iotas(shape):
        return (
            lax.broadcasted_iota(jnp.int32, shape, 0),
            lax.broadcasted_iota(jnp.int32, shape, 1),
        )

    def roll(value, amount):
        return value if amount == 0 else pltpu.roll(value, amount, 1)

    sub, lane = iotas((8, LANES))
    bases = toeplitz(2, jnp.bitwise_and(sub - lane + HALF, LANES - 1))
    pieces = []
    for s in range(0, LANES, 8):
        near = jnp.abs(sub + s - lane) <= HALF
        pieces.append(
            jnp.concatenate([jnp.where(near, roll(base, s), 0.0) for base in bases], axis=1)
        )
    time_mat = jnp.concatenate(pieces, axis=0).astype(bf16)

    lanes = round_up(group * width + LANES, LANES)
    sub, lane = iotas((group, lanes))
    difference = lane - sub * width - lax.axis_index("xline") * cols + HALF
    bases = toeplitz(1, jnp.where(difference >= lanes - 64, difference - lanes, difference))
    mine = jnp.logical_and(lane >= sub * width, lane < (sub + 1) * width)
    for part in range(2):
        for y in range(0, cols, 2):
            pair = jnp.concatenate(
                [jnp.where(mine, roll(bases[part], y + dy), 0.0) for dy in range(2)], axis=0
            )
            start = (part * cols + y) * group
            x_mat[start : start + 2 * group, :] = pair[:, : group * width].astype(bf16)

    sub, lane = iotas((8, LANES))
    bases = toeplitz(0, jnp.bitwise_and(lane - sub - rows + HALF, LANES - 1))
    real_first, imag_first = [
        jnp.concatenate(
            [jnp.where(lane < deep, roll(base, j), 0.0) for j in range(0, rows, 8)], axis=0
        )
        for base in bases
    ]
    blank = jnp.zeros((rows, LANES), f32)
    real_first, imag_first = [
        jnp.concatenate([part, blank], axis=1) for part in (real_first, imag_first)
    ]
    real_next, imag_next = pltpu.roll(real_first, deep, 1), pltpu.roll(imag_first, deep, 1)
    base = jnp.concatenate([real_first - imag_next, imag_first + real_next], axis=0)
    i_mat = jnp.concatenate([base, pltpu.roll(base, 2 * deep, 1)], axis=0).astype(bf16)
    i_mat = i_mat[:, : 4 * deep]

    for step in range(deep // group):
        span = group * width
        band = jnp.dot(
            flat[step * span : (step + 1) * span, :],
            time_mat,
            preferred_element_type=f32,
        ).astype(bf16)
        mixed = jnp.dot(x_mat[...], band, preferred_element_type=f32)
        for y in range(cols):
            with_cos = mixed[y * group : (y + 1) * group]
            with_sin = mixed[(cols + y) * group : (cols + y + 1) * group]
            cu, cv = with_cos[:, :LANES], with_cos[:, LANES:]
            su, sv = with_sin[:, :LANES], with_sin[:, LANES:]
            for slot, value in enumerate((cu - sv, su + cv, cu + sv, su - cv)):
                start = (slot * cols + y) * deep + step * group
                cross[start : start + group, :] = value

    half = cols // 2
    for q in range(2):
        for y0 in range(0, half, 2):
            columns = []
            for dy in range(2):
                pieces = []
                for g in range(2):
                    for r in range(2):
                        start = ((q * 2 + r) * cols + y0 + dy + g * half) * deep
                        pieces.append(cross[start : start + deep, :])
                columns.append(jnp.concatenate(pieces, axis=0).astype(bf16))
            total = jnp.dot(i_mat, jnp.concatenate(columns, axis=1), preferred_element_type=f32)
            for g in range(2):
                re = total[g * 2 * rows : g * 2 * rows + rows]
                im = total[g * 2 * rows + rows : (g + 1) * 2 * rows]
                size = jnp.sqrt(re * re + im * im + eps_mag)
                for dy in range(2):
                    out_ref[
                        y0 + dy + g * half, pl.ds(2 * orient + q, rows, stride=pad), :
                    ] = size[:, dy * LANES : (dy + 1) * LANES]


def filter_features(halo, directions, pad):
    _, xlines, rows, cols, samples = halo.shape
    orients = directions.shape[0]
    width = xlines * cols
    sizes = (rows, cols, width, pad, orients)
    return pl.pallas_call(
        functools.partial(filter_kernel, sizes),
        out_shape=jax.ShapeDtypeStruct((cols, rows * pad, samples), f32),
        grid=(orients,),
        in_specs=[
            pl.BlockSpec(memory_space=SMEM),
            pl.BlockSpec(halo.shape, lambda o: (0,) * 5),
        ],
        out_specs=pl.BlockSpec((cols, rows * pad, samples), lambda o: (0, 0, 0)),
        scratch_shapes=[
            pltpu.VMEM((3 * rows * width, samples), bf16),
            pltpu.VMEM((2 * cols * 8, 8 * width), bf16),
            pltpu.VMEM((4 * cols * 3 * rows, samples), f32),
        ],
        compiler_params=pltpu.CompilerParams(vmem_limit_bytes=50 << 20),
        name="filters",
    )(directions, halo)


def split3(value):
    high = value.astype(bf16)
    rest = value - high.astype(f32)
    mid = rest.astype(bf16)
    low = (rest - mid.astype(f32)).astype(bf16)
    return high, mid, low


def column(row):
    return jnp.transpose(jnp.broadcast_to(row, (row.shape[1], row.shape[1])))


def padded(value, fill):
    comps, count = value.shape
    return jnp.concatenate([value, jnp.full((comps, LANES - count), fill, f32)], axis=1)


def first_params(mean_ref, var_ref, weight_ref):
    comps = mean_ref.shape[0]
    means = padded(mean_ref[...], 0.0)
    shift_row = jnp.mean(means, axis=0, keepdims=True)
    weights = column(padded(weight_ref[...], 1.0))[:comps]
    return (means - shift_row, padded(var_ref[...], 1.0), weights), shift_row


def next_params(folded, params, sizes):
    pad, count, cells = sizes
    means, spreads, _ = params
    comps = means.shape[0]
    total = jnp.concatenate([folded, pltpu.roll(folded, LANES // 2, 1)], axis=0)
    used = lax.broadcasted_iota(jnp.int32, (comps, LANES), 1) < count
    mass = total[:, count : count + 1]
    first = jnp.where(used, total, 0.0)
    second = jnp.where(used, pltpu.roll(total, LANES - pad, 1), 0.0)
    below = mass + 1.0
    new_means = (first + means) / below
    centred = second - 2.0 * new_means * first + new_means * new_means * mass
    new_spreads = jnp.where(used, (centred + spreads) / below, 1.0)
    return new_means, new_spreads, jnp.broadcast_to(below / (cells + comps), (comps, LANES))


def peer(shift, inlines, xlines):
    me = lax.axis_index("inline") * xlines + lax.axis_index("xline")
    other = lax.rem(me + shift, inlines * xlines)
    return {"inline": other // xlines, "xline": lax.rem(other, xlines)}


def greet(inlines, xlines):
    barrier = pltpu.get_barrier_semaphore()
    for shift in range(1, inlines * xlines):
        pl.semaphore_signal(
            barrier, inc=1, device_id=peer(shift, inlines, xlines), device_id_type=MESH
        )


def gather_sum(inlines, xlines, payload_ref, slots, send_sem, recv_sem):
    members = inlines * xlines
    me = lax.axis_index("inline") * xlines + lax.axis_index("xline")
    pl.semaphore_wait(pltpu.get_barrier_semaphore(), members - 1)

    def copy(shift):
        return pltpu.make_async_remote_copy(
            src_ref=payload_ref,
            dst_ref=slots.at[me],
            send_sem=send_sem.at[shift],
            recv_sem=recv_sem.at[shift],
            device_id=peer(shift, inlines, xlines),
            device_id_type=MESH,
        )

    for shift in range(1, members):
        copy(shift).start()
    slots[me] = payload_ref[...]
    for shift in range(1, members):
        copy(shift).wait()
    total = slots[0]
    for member in range(1, members):
        total = total + slots[member]
    return total


def gather_scratch(members, comps):
    return [
        pltpu.VMEM((members, comps // 2, LANES), f32),
        pltpu.SemaphoreType.DMA((members,)),
        pltpu.SemaphoreType.DMA((members,)),
    ]


def moment_kernel(sizes, last, *refs):
    cols, pad, count, chunk, together, cells, inlines, xlines = sizes
    if last:
        feat_ref, sum_ref, mean_ref, var_ref, weight_ref, *refs = refs
        moment_ref, post_ref, shift_ref, table, total, wide = refs
    else:
        feat_ref, mean_ref, var_ref, weight_ref, *refs = refs
        moment_ref, shift_ref, table, total, payload, slots, send_sem, recv_sem = refs
    step = pl.program_id(0)
    comps = mean_ref.shape[0]

    @pl.when(step == 0)
    def _():
        if not last:
            greet(inlines, xlines)
        params, shift_row = first_params(mean_ref, var_ref, weight_ref)
        if last:
            params = next_params(sum_ref[...], params, (pad, count, cells))
        shift_ref[...] = column(shift_row)[:pad]
        lane = lax.broadcasted_iota(jnp.int32, (comps, 2 * LANES), 1)
        means = jnp.concatenate([params[0], jnp.zeros((comps, LANES), f32)], axis=1)
        spreads = jnp.concatenate([params[1], jnp.ones((comps, LANES), f32)], axis=1)
        used = lane < count
        inverse = jnp.where(used, 1.0 / spreads, 0.0)
        scaled = means * inverse
        terms = jnp.where(used, jnp.log(2.0 * math.pi * spreads) + means * scaled, 0.0)
        constant = jnp.log(params[2][:, :1]) - 0.5 * jnp.sum(terms, axis=1, keepdims=True)
        row = jnp.where(used, scaled, 0.0) + jnp.where(lane == count, constant, 0.0)
        row = row + pltpu.roll(-0.5 * inverse, pad, 1)
        parts = split3(row)
        for index, part in enumerate(parts):
            part = part.astype(f32)
            tiled = part + pltpu.roll(part, 2 * pad, 1) + pltpu.roll(part, 4 * pad, 1)
            table[index * comps : (index + 1) * comps, :] = tiled.astype(bf16)
        total[...] = jnp.zeros_like(total)

    weights = table[:, : 6 * pad]
    for j in range(together):
        for first in range(0, cols, chunk):
            values = jnp.concatenate(
                [
                    feat_ref[first + y, j * pad : (j + 1) * pad, :] - shift_ref[...]
                    for y in range(chunk)
                ],
                axis=1,
            )
            both = jnp.concatenate([values, values * values], axis=0)
            operand = jnp.concatenate(split3(both), axis=0)
            wide_score = jnp.dot(weights, operand, preferred_element_type=f32)
            score = wide_score[:comps] + (
                wide_score[comps : 2 * comps] + wide_score[2 * comps : 3 * comps]
            )
            exponent = jnp.exp(score - jnp.max(score, axis=0, keepdims=True))
            share = exponent * (1.0 / jnp.sum(exponent, axis=0, keepdims=True))
            high = share.astype(bf16)
            low = (share - high.astype(f32)).astype(bf16)
            total[...] += lax.dot_general(
                jnp.concatenate([high, low], axis=0),
                operand,
                (((1,), (1,)), ((), ())),
                preferred_element_type=f32,
            )
            if last:
                for y in range(chunk):
                    wide[pl.ds((j * comps) * cols + first + y, comps, stride=cols), :] = share[
                        :, y * LANES : (y + 1) * LANES
                    ]
        if last:
            for k in range(comps):
                start = (j * comps + k) * cols
                post_ref[j, k] = wide[start : start + cols, :].astype(bf16)

    @pl.when(step == pl.num_programs(0) - 1)
    def _():
        both = total[:comps] + total[comps:]
        both = jnp.concatenate([both, jnp.zeros((comps, 2 * LANES - 6 * pad), f32)], axis=1)
        summed = (
            both
            + pltpu.roll(both, 2 * LANES - 2 * pad, 1)
            + pltpu.roll(both, 2 * LANES - 4 * pad, 1)
        )[:, :LANES]
        lane = lax.broadcasted_iota(jnp.int32, (comps, LANES), 1)
        summed = jnp.where(lane < 2 * pad, summed, 0.0)
        half = comps // 2
        folded = summed[:half] + pltpu.roll(summed[half:], LANES // 2, 1)
        if last:
            moment_ref[...] = folded
        else:
            payload[...] = folded
            moment_ref[...] = gather_sum(inlines, xlines, payload, slots, send_sem, recv_sem)


def moments(features, summed, init, count, rows, cells):
    last = summed is not None
    inlines, xlines = lax.axis_size("inline"), lax.axis_size("xline")
    comps = init[0].shape[0]
    cols, flat, samples = features.shape
    pad = flat // rows
    assert 4 * pad <= LANES and comps % 16 == 0
    chunk = 4
    together = 2
    folded = jax.ShapeDtypeStruct((comps // 2, LANES), f32)
    inputs = ([summed] if last else []) + list(init)
    out_shape, out_specs = [folded], [pl.BlockSpec(folded.shape, lambda j: (0, 0))]
    scratch = [
        pltpu.VMEM((pad, LANES), f32),
        pltpu.VMEM((3 * comps, 2 * LANES), bf16),
        pltpu.VMEM((2 * comps, 6 * pad), f32),
    ]
    params = dict(vmem_limit_bytes=50 << 20)
    if last:
        out_shape.append(jax.ShapeDtypeStruct((rows, comps, cols, samples), bf16))
        out_specs.append(pl.BlockSpec((together, comps, cols, samples), lambda j: (j, 0, 0, 0)))
        scratch.append(pltpu.VMEM((together * comps * cols, samples), f32))
    else:
        scratch.append(pltpu.VMEM(folded.shape, f32))
        scratch += gather_scratch(inlines * xlines, comps)
        params.update(collective_id=1, has_side_effects=True)
    sizes = (cols, pad, count, chunk, together, cells, inlines, xlines)
    return pl.pallas_call(
        functools.partial(moment_kernel, sizes, last),
        out_shape=out_shape,
        grid=(rows // together,),
        in_specs=[pl.BlockSpec((cols, together * pad, samples), lambda j: (0, j, 0))]
        + [pl.BlockSpec(array.shape, lambda j: (0, 0)) for array in inputs],
        out_specs=out_specs,
        scratch_shapes=scratch,
        compiler_params=pltpu.CompilerParams(**params),
        name="last_pass" if last else "first_pass",
    )(features, *inputs)


def sum_kernel(inlines, xlines, moment_ref, out_ref, slots, send_sem, recv_sem):
    greet(inlines, xlines)
    out_ref[...] = gather_sum(inlines, xlines, moment_ref, slots, send_sem, recv_sem)


def sum_moments(moment):
    inlines, xlines = lax.axis_size("inline"), lax.axis_size("xline")
    return pl.pallas_call(
        functools.partial(sum_kernel, inlines, xlines),
        out_shape=jax.ShapeDtypeStruct(moment.shape, f32),
        in_specs=[pl.BlockSpec(memory_space=VMEM)],
        out_specs=pl.BlockSpec(memory_space=VMEM),
        scratch_shapes=gather_scratch(inlines * xlines, 2 * moment.shape[0]),
        compiler_params=pltpu.CompilerParams(collective_id=2, has_side_effects=True),
        name="sum_moments",
    )(moment)


def final_kernel(sizes, *refs):
    *sums, mean_ref, var_ref, weight_ref, mean_out, var_out, weight_out = refs
    count = sizes[1]
    params, shift_row = first_params(mean_ref, var_ref, weight_ref)
    for summed in sums:
        params = next_params(summed[...], params, sizes)
    means, spreads, weights = params
    comps = means.shape[0]
    mean_out[...] = (means + shift_row)[:, :count]
    var_out[...] = spreads[:, :count]
    square = jnp.concatenate([weights, jnp.zeros((LANES - comps, LANES), f32)], axis=0)
    weight_out[...] = jnp.transpose(square)[:1, :comps]


def finish(sums, init, sizes):
    comps, count = init[0].shape
    inputs = sums + list(init)
    return pl.pallas_call(
        functools.partial(final_kernel, sizes),
        out_shape=[
            jax.ShapeDtypeStruct((comps, count), f32),
            jax.ShapeDtypeStruct((comps, count), f32),
            jax.ShapeDtypeStruct((1, comps), f32),
        ],
        in_specs=[pl.BlockSpec(memory_space=VMEM)] * len(inputs),
        out_specs=[pl.BlockSpec(memory_space=VMEM)] * 3,
        name="finish",
    )(*inputs)


def per_device(traces, directions, init_means, init_variances, init_weights):
    rows, cols, samples = traces.shape
    assert samples == LANES and rows >= HALF and rows % 8 == 0 and cols % 4 == 0
    count = 2 * directions.shape[0]
    pad = round_up(count + 1, 8)
    comps = init_weights.shape[0]
    cells = lax.axis_size("inline") * rows * lax.axis_size("xline") * cols * samples
    init = (init_means, init_variances, init_weights.reshape(1, comps))
    halo = gather_halo(traces)
    features = filter_features(halo, directions, pad)
    (summed,) = moments(features, None, init, count, rows, cells)
    moment, posterior = moments(features, summed, init, count, rows, cells)
    sums = [summed, sum_moments(moment)]
    means, spreads, weights = finish(sums, init, (pad, count, cells))
    return posterior, means, spreads, weights.reshape(comps)


def solution(mesh):
    in_specs = (P(("slab", "inline"), "xline", None), P(), P(), P(), P())
    out_specs = (
        P(("slab", "inline"), None, "xline", None),
        P("slab", None),
        P("slab", None),
        P("slab"),
    )
    return jax.shard_map(
        per_device, mesh=mesh, in_specs=in_specs, out_specs=out_specs, check_vma=False
    )
```

time: 112 us -> 91.3 us (0.82); the launches traced: 110 us -> 90.7 us
  Pallas kernels: 94.1 us -> 83.3 us
  other arithmetic: 4.21 us -> 0 us
  local copies, waits for them, and re-layouts: 10.4 us -> 6.7 us
    pallas_call x4, Pallas kernels: 58.2 us -> 50.8 us  [the longest x2 40.1 us: moments(): pl.pallas_call(functools.partial(moment_kernel, sizes, last), out_shape=o...]
    pallas_call x1, Pallas kernels: 13.8 us -> 9.88 us  [gather_halo(): pl.pallas_call(functools.partial(halo_kernel, inlines, xlines), out_shape...]
    reduce_sum x2 -> x0, other arithmetic: 1.44 us -> none  [the longest x1 0.82 us: per_device(): shift_row = jnp.mean(init_means, axis=0)]
    unnamed x20 -> x18, local copies, waits for them, and re-layouts: 8.05 us -> 6.7 us
    slice x1 -> x0, local copies, waits for them, and re-layouts: 1.34 us -> none  [per_device(): weights[:, 0]]
where the time goes in v3:
time: 91.3 us; the launch traced here: 90.7 us
  Pallas kernels  83.3 us (91%)
  local copies, waits for them, and re-layouts  6.7 us (7%)
    pallas_call x2, Pallas kernels, moments(): pl.pallas_call(functools.partial(moment_kernel, sizes, last), out_shape=o...  40.1 us
    pallas_call x1, Pallas kernels, filter_features(): pl.pallas_call(functools.partial(filter_kernel, sizes), out_shape=jax.Sha...  22.6 us
    pallas_call x1, Pallas kernels, gather_halo(): pl.pallas_call(functools.partial(halo_kernel, inlines, xlines), out_shape...  9.88 us
    pallas_call x1, Pallas kernels, sum_moments(): pl.pallas_call(functools.partial(sum_kernel, inlines, xlines), out_shape=...  9.17 us
    unnamed x18, local copies, waits for them, and re-layouts  6.7 us

profile of v3, /device:TPU:0, one launch (start us, length us, event | category | flops | bytes accessed | tf_op | source)
XLA Modules:
  0.0 90.7 jit_solution(4199971186641908000)
XLA Ops:
  0.6 0.0 copy-start.5
  0.6 0.8 copy.9.refs_1_.refs_2_
  1.4 0.0 copy-start.1
  1.4 0.8 copy.10.refs_2_.refs_3_
  2.2 0.0 copy-start.2
  2.2 9.9 %halo.1.halo_ref = bf16[3,2,16,24,128]{4,3,2,1,0:T(8,128)(2,1)} custom-call(bf16[16,24,128]{2,1,0:T(8,128)(2,1)} %own_ref.1), custom_call_target="tpu_custom_call" | custom-call | tf_op jit(solution)/shard_map/halo/pallas_call | solution.py:107
  12.1 0.0 copy-start
  12.1 1.1 %copy-done = bf16[3,2,16,24,128]{4,3,2,1,0:T(8,128)(2,1)S(1)} copy-done((bf16[3,2,16,24,128]{4,3,2,1,0:T(8,128)(2,1)S(1)}, bf16[3,2,16,24,128]{4,3,2,1,0:T(8,128)(2,1)}, u32[]{:S(2)}) %copy-start) | copy-done | bytes 589848
  13.2 0.0 copy-start.6
  13.2 0.7 copy-done.6
  13.8 22.6 %filters.1.refs_0_ = f32[24,384,128]{2,1,0:T(8,128)} custom-call(s32[10]{0:T(128)S(1)} %copy-done.6, bf16[3,2,16,24,128]{4,3,2,1,0:T(8,128)(2,1)S(1)} %copy-done), custom_call_target="tpu_custom_call" | custom-call | tf_op jit(solution)/shard_map/filters/pallas_call | solution.py:255
  36.5 0.0 copy-done.5
  36.5 22.9 %first_pass.1.refs_1_.refs_0_ = f32[16,128]{1,0:T(8,128)S(1)} custom-call(f32[24,384,128]{2,1,0:T(8,128)} %filters.1.refs_0_, f32[32,20]{1,0:T(8,128)S(1)} %copy.9.refs_1_.refs_2_, f32[32,20]{1,0:T(8,128)S(1)} %copy.10.refs_2_.refs_3_, f32[1,32]{1,0:T(1,128)S(1)} %bitcast.3), custom_call_target="tpu_custom_call" | custom-call | tf_op jit(solution)/shard_map/first_pass/pallas_call | solution.py:482
  59.4 0.0 copy-done.1
  59.4 0.0 copy-done.2
  59.4 0.0 copy-start.3
  59.4 17.1 %last_pass.1 = (f32[16,128]{1,0:T(8,128)S(1)}, bf16[16,32,24,128]{3,2,1,0:T(8,128)(2,1)}) custom-call(f32[24,384,128]{2,1,0:T(8,128)} %filters.1.refs_0_, f32[16,128]{1,0:T(8,128)S(1)} %first_pass.1.refs_1_.refs_0_, f32[32,20]{1,0:T(8,128)S(1)} %copy.9.refs_1_.refs_2_, f32[32,20]{1,0:T(8,128)S(1)} %copy.10.refs_2_.refs_3_, f32[1,32]{1,0:T(1,128)S(1)} %bitcast.4), custom_call_target="tpu_custom_call" | custom-call | tf_op jit(solution)/shard_map/last_pass/pallas_call | solution.py:482
  76.6 0.0 copy-start.4
  76.6 0.6 copy-done.4
  77.2 9.2 %sum_moments.1.refs_1_ = f32[16,128]{1,0:T(8,128)} custom-call(f32[16,128]{1,0:T(8,128)} %copy-done.4), custom_call_target="tpu_custom_call" | custom-call | tf_op jit(solution)/shard_map/sum_moments/pallas_call | solution.py:502
  86.4 0.0 copy-done.3
  86.4 1.5 %finish.1 = (f32[32,20]{1,0:T(8,128)}, f32[32,20]{1,0:T(8,128)}, f32[1,32]{1,0:T(1,128)}) custom-call(f32[16,128]{1,0:T(8,128)} %copy-done.3, f32[16,128]{1,0:T(8,128)} %sum_moments.1.refs_1_, f32[32,20]{1,0:T(8,128)} %copy-done.1, f32[32,20]{1,0:T(8,128)} %copy-done.2, f32[1,32]{1,0:T(1,128)} %bitcast.2), custom_call_target="tpu_custom_call" | custom-call | tf_op jit(solution)/shard_map/finish/pallas_call | solution.py:530
  87.9 1.4 %copy.15 = f32[32,20]{0,1:T(8,128)} copy(f32[32,20]{1,0:T(8,128)} %get-tuple-element.15) | data formatting | bytes 5120
  89.3 1.4 %copy.16 = f32[32,20]{0,1:T(8,128)} copy(f32[32,20]{1,0:T(8,128)} %get-tuple-element.16) | data formatting | bytes 5120
Async XLA Ops:
  0.6 35.8 %copy-start.5 = (f32[32]{0:T(128)S(1)}, f32[32]{0:T(128)}, u32[]{:S(2)}) copy-start(f32[32]{0:T(128)} %param.9) | copy-start | bytes 388
  1.4 58.0 %copy-start.1 = (f32[32,20]{1,0:T(8,128)}, f32[32,20]{1,0:T(8,128)S(1)}, u32[]{:S(2)}) copy-start(f32[32,20]{1,0:T(8,128)S(1)} %copy.9.refs_1_.refs_2_) | copy-start | bytes 7684
  2.2 57.2 %copy-start.2 = (f32[32,20]{1,0:T(8,128)}, f32[32,20]{1,0:T(8,128)S(1)}, u32[]{:S(2)}) copy-start(f32[32,20]{1,0:T(8,128)S(1)} %copy.10.refs_2_.refs_3_) | copy-start | bytes 7684
  12.1 1.1 %copy-start = (bf16[3,2,16,24,128]{4,3,2,1,0:T(8,128)(2,1)S(1)}, bf16[3,2,16,24,128]{4,3,2,1,0:T(8,128)(2,1)}, u32[]{:S(2)}) copy-start(bf16[3,2,16,24,128]{4,3,2,1,0:T(8,128)(2,1)} %halo.1.halo_ref) | copy-start | bytes 1769476
  13.2 0.7 copy-start.6
  59.4 26.9 %copy-start.3 = (f32[16,128]{1,0:T(8,128)}, f32[16,128]{1,0:T(8,128)S(1)}, u32[]{:S(2)}) copy-start(f32[16,128]{1,0:T(8,128)S(1)} %first_pass.1.refs_1_.refs_0_) | copy-start | bytes 24580
  76.6 0.6 copy-start.4

commit v4 on v3

--- a/solution.py
+++ b/solution.py
@@ -113,7 +113,9 @@
             pltpu.SemaphoreType.DMA((3, xlines)),
             pltpu.SemaphoreType.DMA((3, xlines)),
         ],
-        compiler_params=pltpu.CompilerParams(collective_id=0, has_side_effects=True),
+        compiler_params=pltpu.CompilerParams(
+            collective_id=0, has_side_effects=True, vmem_limit_bytes=4 << 20
+        ),
         name="halo",
     )(traces)
 
@@ -258,15 +260,15 @@
         grid=(orients,),
         in_specs=[
             pl.BlockSpec(memory_space=SMEM),
-            pl.BlockSpec(halo.shape, lambda o: (0,) * 5),
+            pl.BlockSpec(memory_space=VMEM),
         ],
-        out_specs=pl.BlockSpec((cols, rows * pad, samples), lambda o: (0, 0, 0)),
+        out_specs=pl.BlockSpec(memory_space=VMEM),
         scratch_shapes=[
             pltpu.VMEM((3 * rows * width, samples), bf16),
             pltpu.VMEM((2 * cols * 8, 8 * width), bf16),
             pltpu.VMEM((4 * cols * 3 * rows, samples), f32),
         ],
-        compiler_params=pltpu.CompilerParams(vmem_limit_bytes=50 << 20),
+        compiler_params=pltpu.CompilerParams(vmem_limit_bytes=20 << 20),
         name="filters",
     )(directions, halo)
 
@@ -284,16 +286,18 @@
 
 
 def padded(value, fill):
-    comps, count = value.shape
-    return jnp.concatenate([value, jnp.full((comps, LANES - count), fill, f32)], axis=1)
+    rows, lanes = value.shape
+    wide = jnp.concatenate([value, jnp.full((rows, LANES - lanes), fill, f32)], axis=1)
+    full = jnp.concatenate([wide, jnp.full((LANES - rows, LANES), fill, f32)], axis=0)
+    return jnp.transpose(full)
 
 
 def first_params(mean_ref, var_ref, weight_ref):
-    comps = mean_ref.shape[0]
-    means = padded(mean_ref[...], 0.0)
+    comps = mean_ref.shape[1]
+    means = padded(mean_ref[...], 0.0)[:comps]
     shift_row = jnp.mean(means, axis=0, keepdims=True)
-    weights = column(padded(weight_ref[...], 1.0))[:comps]
-    return (means - shift_row, padded(var_ref[...], 1.0), weights), shift_row
+    weights = jnp.broadcast_to(padded(weight_ref[...], 1.0)[:comps, :1], (comps, LANES))
+    return (means - shift_row, padded(var_ref[...], 1.0)[:comps], weights), shift_row
 
 
 def next_params(folded, params, sizes):
@@ -363,13 +367,13 @@
 def moment_kernel(sizes, last, *refs):
     cols, pad, count, chunk, together, cells, inlines, xlines = sizes
     if last:
-        feat_ref, sum_ref, mean_ref, var_ref, weight_ref, *refs = refs
-        moment_ref, post_ref, shift_ref, table, total, wide = refs
+        split_ref, sum_ref, mean_ref, var_ref, weight_ref, *refs = refs
+        moment_ref, post_ref, table, total, wide = refs
     else:
         feat_ref, mean_ref, var_ref, weight_ref, *refs = refs
-        moment_ref, shift_ref, table, total, payload, slots, send_sem, recv_sem = refs
+        moment_ref, split_ref, table, total, shift_ref, payload, slots, send_sem, recv_sem = refs
     step = pl.program_id(0)
-    comps = mean_ref.shape[0]
+    comps = mean_ref.shape[1]
 
     @pl.when(step == 0)
     def _():
@@ -378,7 +382,8 @@
         params, shift_row = first_params(mean_ref, var_ref, weight_ref)
         if last:
             params = next_params(sum_ref[...], params, (pad, count, cells))
-        shift_ref[...] = column(shift_row)[:pad]
+        else:
+            shift_ref[...] = column(shift_row)[:pad]
         lane = lax.broadcasted_iota(jnp.int32, (comps, 2 * LANES), 1)
         means = jnp.concatenate([params[0], jnp.zeros((comps, LANES), f32)], axis=1)
         spreads = jnp.concatenate([params[1], jnp.ones((comps, LANES), f32)], axis=1)
@@ -399,15 +404,21 @@
     weights = table[:, : 6 * pad]
     for j in range(together):
         for first in range(0, cols, chunk):
-            values = jnp.concatenate(
-                [
-                    feat_ref[first + y, j * pad : (j + 1) * pad, :] - shift_ref[...]
-                    for y in range(chunk)
-                ],
-                axis=1,
-            )
-            both = jnp.concatenate([values, values * values], axis=0)
-            operand = jnp.concatenate(split3(both), axis=0)
+            span = slice(first * LANES, (first + chunk) * LANES)
+            if last:
+                operand = split_ref[j, :, span]
+            else:
+                base = pl.multiple_of((step * together + j) * pad, 8)
+                values = jnp.concatenate(
+                    [
+                        feat_ref[first + y, pl.ds(base, pad), :] - shift_ref[...]
+                        for y in range(chunk)
+                    ],
+                    axis=1,
+                )
+                both = jnp.concatenate([values, values * values], axis=0)
+                operand = jnp.concatenate(split3(both), axis=0)
+                split_ref[j, :, span] = operand
             wide_score = jnp.dot(weights, operand, preferred_element_type=f32)
             score = wide_score[:comps] + (
                 wide_score[comps : 2 * comps] + wide_score[2 * comps : 3 * comps]
@@ -452,10 +463,10 @@
             moment_ref[...] = gather_sum(inlines, xlines, payload, slots, send_sem, recv_sem)
 
 
-def moments(features, summed, init, count, rows, cells):
+def moments(features, split, summed, init, count, rows, cells):
     last = summed is not None
     inlines, xlines = lax.axis_size("inline"), lax.axis_size("xline")
-    comps = init[0].shape[0]
+    comps = init[0].shape[1]
     cols, flat, samples = features.shape
     pad = flat // rows
     assert 4 * pad <= LANES and comps % 16 == 0
@@ -464,18 +475,21 @@
     folded = jax.ShapeDtypeStruct((comps // 2, LANES), f32)
     inputs = ([summed] if last else []) + list(init)
     out_shape, out_specs = [folded], [pl.BlockSpec(folded.shape, lambda j: (0, 0))]
+    split_shape = (rows, 6 * pad, cols * samples)
+    split_spec = pl.BlockSpec((together,) + split_shape[1:], lambda j: (j, 0, 0))
     scratch = [
-        pltpu.VMEM((pad, LANES), f32),
         pltpu.VMEM((3 * comps, 2 * LANES), bf16),
         pltpu.VMEM((2 * comps, 6 * pad), f32),
     ]
-    params = dict(vmem_limit_bytes=50 << 20)
+    params = dict(vmem_limit_bytes=24 << 20)
     if last:
         out_shape.append(jax.ShapeDtypeStruct((rows, comps, cols, samples), bf16))
         out_specs.append(pl.BlockSpec((together, comps, cols, samples), lambda j: (j, 0, 0, 0)))
         scratch.append(pltpu.VMEM((together * comps * cols, samples), f32))
     else:
-        scratch.append(pltpu.VMEM(folded.shape, f32))
+        out_shape.append(jax.ShapeDtypeStruct(split_shape, bf16))
+        out_specs.append(split_spec)
+        scratch += [pltpu.VMEM((pad, LANES), f32), pltpu.VMEM(folded.shape, f32)]
         scratch += gather_scratch(inlines * xlines, comps)
         params.update(collective_id=1, has_side_effects=True)
     sizes = (cols, pad, count, chunk, together, cells, inlines, xlines)
@@ -483,13 +497,13 @@
         functools.partial(moment_kernel, sizes, last),
         out_shape=out_shape,
         grid=(rows // together,),
-        in_specs=[pl.BlockSpec((cols, together * pad, samples), lambda j: (0, j, 0))]
+        in_specs=[split_spec if last else pl.BlockSpec(memory_space=VMEM)]
         + [pl.BlockSpec(array.shape, lambda j: (0, 0)) for array in inputs],
         out_specs=out_specs,
         scratch_shapes=scratch,
         compiler_params=pltpu.CompilerParams(**params),
         name="last_pass" if last else "first_pass",
-    )(features, *inputs)
+    )(split if last else features, *inputs)
 
 
 def sum_kernel(inlines, xlines, moment_ref, out_ref, slots, send_sem, recv_sem):
@@ -505,7 +519,9 @@
         in_specs=[pl.BlockSpec(memory_space=VMEM)],
         out_specs=pl.BlockSpec(memory_space=VMEM),
         scratch_shapes=gather_scratch(inlines * xlines, 2 * moment.shape[0]),
-        compiler_params=pltpu.CompilerParams(collective_id=2, has_side_effects=True),
+        compiler_params=pltpu.CompilerParams(
+            collective_id=2, has_side_effects=True, vmem_limit_bytes=4 << 20
+        ),
         name="sum_moments",
     )(moment)
 
@@ -518,24 +534,29 @@
         params = next_params(summed[...], params, sizes)
     means, spreads, weights = params
     comps = means.shape[0]
-    mean_out[...] = (means + shift_row)[:, :count]
-    var_out[...] = spreads[:, :count]
-    square = jnp.concatenate([weights, jnp.zeros((LANES - comps, LANES), f32)], axis=0)
-    weight_out[...] = jnp.transpose(square)[:1, :comps]
+    blank = jnp.zeros((LANES - comps, LANES), f32)
+    turned = [
+        jnp.transpose(jnp.concatenate([value, blank], axis=0))[:, :comps]
+        for value in (means + shift_row, spreads, weights)
+    ]
+    mean_out[...] = turned[0][:count]
+    var_out[...] = turned[1][:count]
+    weight_out[...] = turned[2][:1]
 
 
 def finish(sums, init, sizes):
-    comps, count = init[0].shape
+    count, comps = init[0].shape
     inputs = sums + list(init)
     return pl.pallas_call(
         functools.partial(final_kernel, sizes),
         out_shape=[
-            jax.ShapeDtypeStruct((comps, count), f32),
-            jax.ShapeDtypeStruct((comps, count), f32),
+            jax.ShapeDtypeStruct((count, comps), f32),
+            jax.ShapeDtypeStruct((count, comps), f32),
             jax.ShapeDtypeStruct((1, comps), f32),
         ],
         in_specs=[pl.BlockSpec(memory_space=VMEM)] * len(inputs),
         out_specs=[pl.BlockSpec(memory_space=VMEM)] * 3,
+        compiler_params=pltpu.CompilerParams(vmem_limit_bytes=4 << 20),
         name="finish",
     )(*inputs)
 
@@ -547,14 +568,14 @@
     pad = round_up(count + 1, 8)
     comps = init_weights.shape[0]
     cells = lax.axis_size("inline") * rows * lax.axis_size("xline") * cols * samples
-    init = (init_means, init_variances, init_weights.reshape(1, comps))
+    init = (init_means.T, init_variances.T, init_weights.reshape(1, comps))
     halo = gather_halo(traces)
     features = filter_features(halo, directions, pad)
-    (summed,) = moments(features, None, init, count, rows, cells)
-    moment, posterior = moments(features, summed, init, count, rows, cells)
+    summed, split = moments(features, None, None, init, count, rows, cells)
+    moment, posterior = moments(features, split, summed, init, count, rows, cells)
     sums = [summed, sum_moments(moment)]
     means, spreads, weights = finish(sums, init, (pad, count, cells))
-    return posterior, means, spreads, weights.reshape(comps)
+    return posterior, means.T, spreads.T, weights.reshape(comps)
 
 
 def solution(mesh):

time: 91.3 us -> 77.7 us (0.85)
  Pallas kernels: 83.3 us -> 75.2 us
  local copies, waits for them, and re-layouts: 6.7 us -> 1.56 us
    unnamed x18 -> x10, local copies, waits for them, and re-layouts: 6.7 us -> 1.56 us
    pallas_call x2, Pallas kernels: 40.1 us -> 37.8 us  [moments(): pl.pallas_call(functools.partial(moment_kernel, sizes, last), out_shape=o...]
    pallas_call x1, Pallas kernels: 22.6 us -> 20.5 us  [filter_features(): pl.pallas_call(functools.partial(filter_kernel, sizes), out_shape=jax.Sha...]
    pallas_call x1, Pallas kernels: 9.88 us -> 8.16 us  [gather_halo(): pl.pallas_call(functools.partial(halo_kernel, inlines, xlines), out_shape...]
    pallas_call x1, Pallas kernels: 9.17 us -> 7.92 us  [sum_moments(): pl.pallas_call(functools.partial(sum_kernel, inlines, xlines), out_shape=...]
where the time goes in v4:
time: 77.7 us; the launch traced here: 77.5 us
  Pallas kernels  75.2 us (97%)
  local copies, waits for them, and re-layouts  1.56 us (2%)
    pallas_call x2, Pallas kernels, moments(): pl.pallas_call(functools.partial(moment_kernel, sizes, last), out_shape=o...  37.8 us
    pallas_call x1, Pallas kernels, filter_features(): pl.pallas_call(functools.partial(filter_kernel, sizes), out_shape=jax.Sha...  20.5 us
    pallas_call x1, Pallas kernels, gather_halo(): pl.pallas_call(functools.partial(halo_kernel, inlines, xlines), out_shape...  8.16 us
    pallas_call x1, Pallas kernels, sum_moments(): pl.pallas_call(functools.partial(sum_kernel, inlines, xlines), out_shape=...  7.92 us
    unnamed x10, local copies, waits for them, and re-layouts  1.56 us

profile of v4, /device:TPU:0, one launch (start us, length us, event | category | flops | bytes accessed | tf_op | source)
XLA Modules:
  0.0 77.5 jit_solution(2188952147083341734)
XLA Ops:
  0.6 0.0 copy-start.1
  0.6 0.0 copy-start
  0.7 0.0 copy-start.2
  0.7 0.9 %copy-done.2 = bf16[16,24,128]{2,1,0:T(8,128)(2,1)S(1)} copy-done((bf16[16,24,128]{2,1,0:T(8,128)(2,1)S(1)}, bf16[16,24,128]{2,1,0:T(8,128)(2,1)}, u32[]{:S(2)}) %copy-start.2) | copy-done | bytes 98328
  1.6 0.0 copy-start.3
  1.6 8.2 %halo.1.halo_ref = bf16[3,2,16,24,128]{4,3,2,1,0:T(8,128)(2,1)S(1)} custom-call(bf16[16,24,128]{2,1,0:T(8,128)(2,1)S(1)} %copy-done.2), custom_call_target="tpu_custom_call" | custom-call | tf_op jit(solution)/shard_map/halo/pallas_call | solution.py:107
  9.7 0.0 copy-start.4
  9.7 0.6 copy-done.4
  10.4 20.5 %filters.1.refs_0_ = f32[24,384,128]{2,1,0:T(8,128)S(1)} custom-call(s32[10]{0:T(128)S(1)} %copy-done.4, bf16[3,2,16,24,128]{4,3,2,1,0:T(8,128)(2,1)S(1)} %halo.1.halo_ref), custom_call_target="tpu_custom_call" | custom-call | tf_op jit(solution)/shard_map/filters/pallas_call | solution.py:257
  30.9 0.0 copy-done.1
  30.9 0.0 copy-done
  30.9 0.0 copy-done.3
  30.9 22.1 %first_pass.1 = (f32[16,128]{1,0:T(8,128)S(1)}, bf16[16,144,3072]{2,1,0:T(8,128)(2,1)S(1)}) custom-call(f32[24,384,128]{2,1,0:T(8,128)S(1)} %filters.1.refs_0_, f32[20,32]{1,0:T(8,128)S(1)} %bitcast.6, f32[20,32]{1,0:T(8,128)S(1)} %bitcast.9, f32[1,32]{1,0:T(1,128)S(1)} %bitcast.12), custom_call_target="tpu_custom_call" | custom-call | tf_op jit(solution)/shard_map/first_pass/pallas_call | solution.py:496
  53.0 15.7 %last_pass.1 = (f32[16,128]{1,0:T(8,128)S(1)}, bf16[16,32,24,128]{3,2,1,0:T(8,128)(2,1)}) custom-call(bf16[16,144,3072]{2,1,0:T(8,128)(2,1)S(1)} %get-tuple-element.11.refs_0_, f32[16,128]{1,0:T(8,128)S(1)} %get-tuple-element.12.refs_1_.refs_0_, f32[20,32]{1,0:T(8,128)S(1)} %bitcast.7, f32[20,32]{1,0:T(8,128)S(1)} %bitcast.10, f32[1,32]{1,0:T(1,128)S(1)} %bitcast.13), custom_call_target="tpu_custom_call" | custom-call | tf_op jit(solution)/shard_map/last_pass/pallas_call | solution.py:496
  68.7 7.9 %sum_moments.1.refs_1_ = f32[16,128]{1,0:T(8,128)S(1)} custom-call(f32[16,128]{1,0:T(8,128)S(1)} %get-tuple-element.14.moment_ref), custom_call_target="tpu_custom_call" | custom-call | tf_op jit(solution)/shard_map/sum_moments/pallas_call | solution.py:516
  76.7 0.8 %finish.1 = (f32[20,32]{1,0:T(8,128)}, f32[20,32]{1,0:T(8,128)}, f32[1,32]{1,0:T(1,128)}) custom-call(f32[16,128]{1,0:T(8,128)S(1)} %get-tuple-element.12.refs_1_.refs_0_, f32[16,128]{1,0:T(8,128)S(1)} %sum_moments.1.refs_1_, f32[20,32]{1,0:T(8,128)S(1)} %bitcast.8, f32[20,32]{1,0:T(8,128)S(1)} %bitcast.11, f32[1,32]{1,0:T(1,128)S(1)} %bitcast.14), custom_call_target="tpu_custom_call" | custom-call | tf_op jit(solution)/shard_map/finish/pallas_call | solution.py:550
Async XLA Ops:
  0.6 30.3 %copy-start.1 = (f32[32,20]{0,1:T(8,128)S(1)}, f32[32,20]{0,1:T(8,128)}, u32[]{:S(2)}) copy-start(f32[32,20]{0,1:T(8,128)} %param.8) | copy-start | bytes 7684
  0.6 30.3 %copy-start = (f32[32,20]{0,1:T(8,128)S(1)}, f32[32,20]{0,1:T(8,128)}, u32[]{:S(2)}) copy-start(f32[32,20]{0,1:T(8,128)} %param.7) | copy-start | bytes 7684
  0.7 0.9 %copy-start.2 = (bf16[16,24,128]{2,1,0:T(8,128)(2,1)S(1)}, bf16[16,24,128]{2,1,0:T(8,128)(2,1)}, u32[]{:S(2)}) copy-start(bf16[16,24,128]{2,1,0:T(8,128)(2,1)} %own_ref.1) | copy-start | bytes 294916
  1.6 29.4 %copy-start.3 = (f32[32]{0:T(128)S(1)}, f32[32]{0:T(128)}, u32[]{:S(2)}) copy-start(f32[32]{0:T(128)} %param.9) | copy-start | bytes 388
  9.7 0.7 copy-start.4

commit v5 on v4

--- a/solution.py
+++ b/solution.py
@@ -402,43 +402,53 @@
         total[...] = jnp.zeros_like(total)
 
     weights = table[:, : 6 * pad]
-    for j in range(together):
-        for first in range(0, cols, chunk):
-            span = slice(first * LANES, (first + chunk) * LANES)
-            if last:
-                operand = split_ref[j, :, span]
-            else:
-                base = pl.multiple_of((step * together + j) * pad, 8)
-                values = jnp.concatenate(
-                    [
-                        feat_ref[first + y, pl.ds(base, pad), :] - shift_ref[...]
-                        for y in range(chunk)
-                    ],
-                    axis=1,
-                )
-                both = jnp.concatenate([values, values * values], axis=0)
-                operand = jnp.concatenate(split3(both), axis=0)
-                split_ref[j, :, span] = operand
-            wide_score = jnp.dot(weights, operand, preferred_element_type=f32)
-            score = wide_score[:comps] + (
-                wide_score[comps : 2 * comps] + wide_score[2 * comps : 3 * comps]
+    def scores(j, first):
+        span = slice(first * LANES, (first + chunk) * LANES)
+        if last:
+            operand = split_ref[j, :, span]
+        else:
+            base = pl.multiple_of((step * together + j) * pad, 8)
+            values = jnp.concatenate(
+                [
+                    feat_ref[first + y, pl.ds(base, pad), :] - shift_ref[...]
+                    for y in range(chunk)
+                ],
+                axis=1,
             )
-            exponent = jnp.exp(score - jnp.max(score, axis=0, keepdims=True))
-            share = exponent * (1.0 / jnp.sum(exponent, axis=0, keepdims=True))
-            high = share.astype(bf16)
-            low = (share - high.astype(f32)).astype(bf16)
-            total[...] += lax.dot_general(
-                jnp.concatenate([high, low], axis=0),
-                operand,
-                (((1,), (1,)), ((), ())),
-                preferred_element_type=f32,
-            )
-            if last:
-                for y in range(chunk):
-                    wide[pl.ds((j * comps) * cols + first + y, comps, stride=cols), :] = share[
-                        :, y * LANES : (y + 1) * LANES
-                    ]
+            both = jnp.concatenate([values, values * values], axis=0)
+            operand = jnp.concatenate(split3(both), axis=0)
+            split_ref[j, :, span] = operand
+        wide_score = jnp.dot(weights, operand, preferred_element_type=f32)
+        score = wide_score[:comps] + (
+            wide_score[comps : 2 * comps] + wide_score[2 * comps : 3 * comps]
+        )
+        return operand, score
+
+    pieces = [(j, first) for j in range(together) for first in range(0, cols, chunk)]
+    ahead = scores(*pieces[0])
+    moment = total[...]
+    for index, (j, first) in enumerate(pieces):
+        operand, score = ahead
+        if index + 1 < len(pieces):
+            ahead = scores(*pieces[index + 1])
+        exponent = jnp.exp(score - jnp.max(score, axis=0, keepdims=True))
+        share = exponent * (1.0 / jnp.sum(exponent, axis=0, keepdims=True))
+        high = share.astype(bf16)
+        low = (share - high.astype(f32)).astype(bf16)
+        moment = moment + lax.dot_general(
+            jnp.concatenate([high, low], axis=0),
+            operand,
+            (((1,), (1,)), ((), ())),
+            preferred_element_type=f32,
+        )
         if last:
+            for y in range(chunk):
+                wide[pl.ds((j * comps) * cols + first + y, comps, stride=cols), :] = share[
+                    :, y * LANES : (y + 1) * LANES
+                ]
+    total[...] = moment
+    if last:
+        for j in range(together):
             for k in range(comps):
                 start = (j * comps + k) * cols
                 post_ref[j, k] = wide[start : start + cols, :].astype(bf16)

time: 77.7 us -> 72.8 us (0.937)
  Pallas kernels: 75.2 us -> 70.3 us
    pallas_call x2, Pallas kernels: 37.8 us -> 32.9 us  [moments(): pl.pallas_call(functools.partial(moment_kernel, sizes, last), out_shape=o...]
where the time goes in v5:
time: 72.8 us; the launch traced here: 72.6 us
  Pallas kernels  70.3 us (97%)
  local copies, waits for them, and re-layouts  1.56 us (2%)
    pallas_call x2, Pallas kernels, moments(): pl.pallas_call(functools.partial(moment_kernel, sizes, last), out_shape=o...  32.9 us
    pallas_call x1, Pallas kernels, filter_features(): pl.pallas_call(functools.partial(filter_kernel, sizes), out_shape=jax.Sha...  20.5 us
    pallas_call x1, Pallas kernels, gather_halo(): pl.pallas_call(functools.partial(halo_kernel, inlines, xlines), out_shape...  8.16 us
    pallas_call x1, Pallas kernels, sum_moments(): pl.pallas_call(functools.partial(sum_kernel, inlines, xlines), out_shape=...  7.93 us
    unnamed x10, local copies, waits for them, and re-layouts  1.56 us

profile of v5, /device:TPU:0, one launch (start us, length us, event | category | flops | bytes accessed | tf_op | source)
XLA Modules:
  0.0 72.6 jit_solution(10874470299792201719)
XLA Ops:
  0.6 0.0 copy-start.1
  0.6 0.0 copy-start
  0.7 0.0 copy-start.2
  0.7 0.9 %copy-done.2 = bf16[16,24,128]{2,1,0:T(8,128)(2,1)S(1)} copy-done((bf16[16,24,128]{2,1,0:T(8,128)(2,1)S(1)}, bf16[16,24,128]{2,1,0:T(8,128)(2,1)}, u32[]{:S(2)}) %copy-start.2) | copy-done | bytes 98328
  1.6 0.0 copy-start.3
  1.6 8.2 %halo.1.halo_ref = bf16[3,2,16,24,128]{4,3,2,1,0:T(8,128)(2,1)S(1)} custom-call(bf16[16,24,128]{2,1,0:T(8,128)(2,1)S(1)} %copy-done.2), custom_call_target="tpu_custom_call" | custom-call | tf_op jit(solution)/shard_map/halo/pallas_call | solution.py:107
  9.7 0.0 copy-start.4
  9.7 0.6 copy-done.4
  10.4 20.5 %filters.1.refs_0_ = f32[24,384,128]{2,1,0:T(8,128)S(1)} custom-call(s32[10]{0:T(128)S(1)} %copy-done.4, bf16[3,2,16,24,128]{4,3,2,1,0:T(8,128)(2,1)S(1)} %halo.1.halo_ref), custom_call_target="tpu_custom_call" | custom-call | tf_op jit(solution)/shard_map/filters/pallas_call | solution.py:257
  30.9 0.0 copy-done.1
  30.9 0.0 copy-done
  30.9 0.0 copy-done.3
  30.9 19.7 %first_pass.1 = (f32[16,128]{1,0:T(8,128)S(1)}, bf16[16,144,3072]{2,1,0:T(8,128)(2,1)S(1)}) custom-call(f32[24,384,128]{2,1,0:T(8,128)S(1)} %filters.1.refs_0_, f32[20,32]{1,0:T(8,128)S(1)} %bitcast.6, f32[20,32]{1,0:T(8,128)S(1)} %bitcast.9, f32[1,32]{1,0:T(1,128)S(1)} %bitcast.12), custom_call_target="tpu_custom_call" | custom-call | tf_op jit(solution)/shard_map/first_pass/pallas_call | solution.py:506
  50.7 13.2 %last_pass.1 = (f32[16,128]{1,0:T(8,128)S(1)}, bf16[16,32,24,128]{3,2,1,0:T(8,128)(2,1)}) custom-call(bf16[16,144,3072]{2,1,0:T(8,128)(2,1)S(1)} %get-tuple-element.11.refs_0_, f32[16,128]{1,0:T(8,128)S(1)} %get-tuple-element.12.refs_1_.refs_0_, f32[20,32]{1,0:T(8,128)S(1)} %bitcast.7, f32[20,32]{1,0:T(8,128)S(1)} %bitcast.10, f32[1,32]{1,0:T(1,128)S(1)} %bitcast.13), custom_call_target="tpu_custom_call" | custom-call | tf_op jit(solution)/shard_map/last_pass/pallas_call | solution.py:506
  63.8 7.9 %sum_moments.1.refs_1_ = f32[16,128]{1,0:T(8,128)S(1)} custom-call(f32[16,128]{1,0:T(8,128)S(1)} %get-tuple-element.14.moment_ref), custom_call_target="tpu_custom_call" | custom-call | tf_op jit(solution)/shard_map/sum_moments/pallas_call | solution.py:526
  71.8 0.8 %finish.1 = (f32[20,32]{1,0:T(8,128)}, f32[20,32]{1,0:T(8,128)}, f32[1,32]{1,0:T(1,128)}) custom-call(f32[16,128]{1,0:T(8,128)S(1)} %get-tuple-element.12.refs_1_.refs_0_, f32[16,128]{1,0:T(8,128)S(1)} %sum_moments.1.refs_1_, f32[20,32]{1,0:T(8,128)S(1)} %bitcast.8, f32[20,32]{1,0:T(8,128)S(1)} %bitcast.11, f32[1,32]{1,0:T(1,128)S(1)} %bitcast.14), custom_call_target="tpu_custom_call" | custom-call | tf_op jit(solution)/shard_map/finish/pallas_call | solution.py:560
Async XLA Ops:
  0.6 30.3 %copy-start.1 = (f32[32,20]{0,1:T(8,128)S(1)}, f32[32,20]{0,1:T(8,128)}, u32[]{:S(2)}) copy-start(f32[32,20]{0,1:T(8,128)} %param.8) | copy-start | bytes 7684
  0.6 30.3 %copy-start = (f32[32,20]{0,1:T(8,128)S(1)}, f32[32,20]{0,1:T(8,128)}, u32[]{:S(2)}) copy-start(f32[32,20]{0,1:T(8,128)} %param.7) | copy-start | bytes 7684
  0.7 0.9 %copy-start.2 = (bf16[16,24,128]{2,1,0:T(8,128)(2,1)S(1)}, bf16[16,24,128]{2,1,0:T(8,128)(2,1)}, u32[]{:S(2)}) copy-start(bf16[16,24,128]{2,1,0:T(8,128)(2,1)} %own_ref.1) | copy-start | bytes 294916
  1.6 29.4 %copy-start.3 = (f32[32]{0:T(128)S(1)}, f32[32]{0:T(128)}, u32[]{:S(2)}) copy-start(f32[32]{0:T(128)} %param.9) | copy-start | bytes 388
  9.7 0.7 copy-start.4
